TPU v7x, 32 devices: a whole 2x2x4 slice. The times are simulated.
32 devices in a mesh: row: 8 (over z, x), col: 4 (over y, core).
Axes of the slice: x: 2, y: 2, z: 4, core: 2. Of those that a mesh axis runs over, the one named last changes fastest.
Arguments:
- resident_inverse: float32 [12288, 12288], P('row', 'col'), as said below
- factor_panel: float32 [2, 12288, 256], P(None, 'row', 'col'), may hold values from -0.109375 to 0.109375
- diag_inverse: float32 [2, 256, 256], P(None, 'row', 'col'), as said below
- ancestors: int32 [2, 48], replicated, may hold values from 0 to 1, as said below
- start_order: int32 [2], replicated, may hold values from 0 to 1, each once
Outputs:
- inverse_column: float32 [2, 12288, 256], P(None, 'row', 'col')
- inverse_row: float32 [2, 256, 12288], P(None, 'row', 'col')
- diagonal_block: float32 [2, 256, 256], P(None, 'row', 'col')
Inputs may be any that keep to these rules, and one draw needn't show every extreme that they name: `ancestors`: 1 marks a tile of 256 rows among the supernode's ancestor rows; each supernode marks between 32 and 48 tiles. `start_order`: a permutation of the supernodes. `resident_inverse`: symmetric. `diag_inverse`: each supernode's block is symmetric.
All inputs are finite; a program needn't handle non-finite values.
Results may differ from a plain program's by a relative error of at most 0.0001.
Values sent between devices are 32-bit elements; how exact they have to be, the bound alone decides.
No kernel may reach another device: no remote copies, remote signals or barrier semaphores. Data moves between devices by JAX's collectives and lax.ppermute only.
A program may use at most 64 MiB of HBM per device.

v0:
```python
import functools
import jax
import jax.numpy as jnp
from jax import lax
from jax.experimental import pallas as pl
from jax.experimental.pallas import tpu as pltpu
from jax.sharding import PartitionSpec as P

INNER = 2


def swap_bit(block, axis, bit):
    count = lax.axis_size(axis)
    return lax.ppermute(block, axis, [(i, i ^ (1 << bit)) for i in range(count)])


def split(values):
    high = values.astype(jnp.bfloat16)
    return high, (values - high.astype(jnp.float32)).astype(jnp.bfloat16)


def dot(left, right, contract):
    return lax.dot_general(left, right, (contract, ((), ())), preferred_element_type=jnp.float32)


def mask_kernel(tile, order_ref, flags_ref, place_ref, panel_ref, out_ref):
    section = order_ref[pl.program_id(0)]
    for t in range(panel_ref.shape[2] // tile):
        flag = flags_ref[section, place_ref[0] + t].astype(jnp.float32)
        at = pl.ds(t * tile, tile)
        out_ref[0, :, at] = panel_ref[0, :, at] * flag


def masked_panels(panel, ancestors, start_order, first_tile, tile):
    sections, width, rows = panel.shape
    return pl.pallas_call(
        functools.partial(mask_kernel, tile),
        grid_spec=pltpu.PrefetchScalarGridSpec(
            num_scalar_prefetch=3,
            grid=(sections,),
            in_specs=[pl.BlockSpec((1, width, rows), lambda s, order, flags, place: (order[s], 0, 0))],
            out_specs=pl.BlockSpec((1, width, rows), lambda s, order, flags, place: (s, 0, 0)),
        ),
        out_shape=jax.ShapeDtypeStruct(panel.shape, jnp.float32),
        compiler_params=pltpu.CompilerParams(vmem_limit_bytes=8 << 20),
        cost_estimate=pl.CostEstimate(flops=panel.size, bytes_accessed=8 * panel.size, transcendentals=0),
        name="mask_panels",
    )(start_order, ancestors, first_tile, panel)


def column_block(columns):
    return next(columns // t for t in range(1, columns + 1) if columns % t == 0 and columns // t <= 512)


def terms_kernel(dims, table_ref, inverse_ref, *refs):
    pieces_count, ratio, narrow, steps, members = dims
    pieces, refs = refs[:pieces_count], refs[pieces_count:]
    sends, (kept_ref, high_ref, low_ref, left_ref) = refs[:steps], refs[steps:]
    h = pl.program_id(0)
    n = pl.program_id(1)
    rows = members * steps * INNER * narrow

    @pl.when((h == 0) & (n == 0))
    def _():
        for m in range(pieces_count):
            for g in range(members):
                for l in range(ratio):
                    high, low = split(pieces[m][g, l * narrow : (l + 1) * narrow, :])
                    high_ref[m * ratio + l, g] = high
                    low_ref[m * ratio + l, g] = low

    @pl.when(n == 0)
    def _():
        for j in range(steps):
            for i in range(INNER):
                unit = table_ref[h, j * INNER + i]
                for g in range(members):
                    at = ((g * steps + j) * INNER + i) * narrow
                    left_ref[at : at + narrow, :] = high_ref[unit, g]
                    left_ref[rows + at : rows + at + narrow, :] = low_ref[unit, g]

    high, low = split(inverse_ref[...])
    both = dot(left_ref[...], high, ((1,), (0,)))
    total = both[:rows] + both[rows:] + dot(left_ref[:rows, :], low, ((1,), (0,)))
    total = total.reshape(members, steps, INNER, narrow, total.shape[1])
    for g in range(members):
        for j in range(steps):
            sends[j][g, 0] = total[g, j, 0]
            kept_ref[j, g, 0] = total[g, j, 1]


def panel_terms(table, inverse, pieces, ratio):
    members, width, rows = pieces[0].shape
    count = len(pieces)
    steps = table.shape[1] // INNER
    narrow = width // ratio
    half = inverse.shape[1] // 2
    block = column_block(half)
    tiles = half // block
    lefts = members * steps * INNER * narrow
    whole = pl.BlockSpec((members, width, rows), lambda h, n, table: (0, 0, 0))
    flops = 6 * lefts * inverse.size
    outs = pl.pallas_call(
        functools.partial(terms_kernel, (count, ratio, narrow, steps, members)),
        grid_spec=pltpu.PrefetchScalarGridSpec(
            num_scalar_prefetch=1,
            grid=(2, tiles),
            in_specs=[pl.BlockSpec((rows, block), lambda h, n, table: (0, h * tiles + n))] + [whole] * count,
            out_specs=[pl.BlockSpec((members, 1, narrow, block), lambda h, n, table: (0, h, 0, n))] * steps
            + [pl.BlockSpec((steps, members, 1, narrow, block), lambda h, n, table: (0, 0, h, 0, n))],
            scratch_shapes=[
                pltpu.VMEM((count * ratio, members, narrow, rows), jnp.bfloat16),
                pltpu.VMEM((count * ratio, members, narrow, rows), jnp.bfloat16),
                pltpu.VMEM((2 * lefts, rows), jnp.bfloat16),
            ],
        ),
        out_shape=[jax.ShapeDtypeStruct((members, 2, narrow, half), jnp.float32)] * steps
        + [jax.ShapeDtypeStruct((steps, members, 2, narrow, half), jnp.float32)],
        compiler_params=pltpu.CompilerParams(vmem_limit_bytes=32 << 20),
        cost_estimate=pl.CostEstimate(flops=flops, bytes_accessed=4 * inverse.size, transcendentals=0),
        name="panel_terms",
    )(table, inverse, *pieces)
    return outs[:steps], outs[steps]


def gather_pieces(block):
    count = lax.axis_size("col")
    pieces = {0: block}
    for bit in reversed(range(count.bit_length() - 1)):
        for held, piece in list(pieces.items()):
            pieces[held ^ (1 << bit)] = swap_bit(piece, "col", bit)
    return [pieces[i] for i in range(count)]


def mirror_routes(row_count, col_count, shift):
    ratio = row_count // col_count
    straight, first, second = [], [], []
    for r in range(row_count):
        for c in range(col_count):
            target = (c * ratio + (r % ratio + shift) % ratio, r // ratio)
            middle = (r, target[1] // 2 * 2 + c % 2)
            if shift == 0 or middle[1] == c:
                straight.append(((r, c), target))
            else:
                first.append(((r, c), middle))
                second.append((middle, target))
    if len(set(m for _, m in first)) != len(first):
        straight += [(f[0], s[1]) for f, s in zip(first, second)]
        first, second = [], []
    flat = lambda pairs: [(a[0] * col_count + a[1], b[0] * col_count + b[1]) for a, b in pairs]
    return flat(straight), flat(first), flat(second)


def mirrored(pieces):
    row_count = lax.axis_size("row")
    col_count = lax.axis_size("col")
    ratio = row_count // col_count
    lower = lax.axis_index("row") % ratio
    arrived = []
    for shift in range(ratio):
        straight, first, second = mirror_routes(row_count, col_count, shift)
        piece = pieces[(0 + shift) % ratio]
        for l in range(1, ratio):
            piece = jnp.where(lower == l, pieces[(l + shift) % ratio], piece)
        got = lax.ppermute(piece, ("row", "col"), straight)
        if first:
            halfway = lax.ppermute(piece, ("row", "col"), first)
            got = got + lax.ppermute(halfway, ("row", "col"), second)
        arrived.append(got)
    return arrived


def unmirror(arrived, axis):
    ratio = len(arrived)
    lower = lax.axis_index("row") % ratio
    placed = []
    for source in range(ratio):
        piece = arrived[(0 - source) % ratio]
        for l in range(1, ratio):
            piece = jnp.where(lower == l, arrived[(l - source) % ratio], piece)
        placed.append(piece)
    return jnp.concatenate(placed, axis=axis)


def diag_kernel(count, column_ref, *refs):
    pieces, out_ref = refs[:count], refs[count]
    width = pieces[0].shape[1]
    for g in range(out_ref.shape[0]):
        high, low = split(column_ref[g])
        for m in range(count):
            left_high, left_low = split(pieces[m][g])
            left = jnp.concatenate([left_high, left_low], axis=0)
            both = dot(left, high, ((1,), (1,)))
            out_ref[g, m] = both[:width] + both[width:] + dot(left_high, low, ((1,), (1,)))


def diag_terms(column, pieces):
    members, width, rows = column.shape
    count = len(pieces)
    return pl.pallas_call(
        functools.partial(diag_kernel, count),
        out_shape=jax.ShapeDtypeStruct((members, count, width, width), jnp.float32),
        compiler_params=pltpu.CompilerParams(vmem_limit_bytes=16 << 20),
        cost_estimate=pl.CostEstimate(
            flops=6 * members * count * width * width * rows,
            bytes_accessed=4 * members * (count + 1) * width * rows,
            transcendentals=0,
        ),
        name="diag_terms",
    )(column, *pieces)


def on_device(resident_inverse, factor_panel, diag_inverse, ancestors, start_order):
    row_count = lax.axis_size("row")
    col_count = lax.axis_size("col")
    row_index = lax.axis_index("row")
    col_index = lax.axis_index("col")
    rows_here, cols_here = resident_inverse.shape
    sections, _, slice_width = factor_panel.shape
    tile = rows_here * row_count // ancestors.shape[1]
    ratio = row_count // col_count
    narrow = slice_width // ratio
    steps = row_count // INNER
    outer = row_index // INNER
    inner = row_index % INNER
    half = cols_here // 2

    first_tile = (row_index * (rows_here // tile)).astype(jnp.int32).reshape(1)
    own = masked_panels(jnp.swapaxes(factor_panel, 1, 2), ancestors, start_order, first_tile, tile)

    tiles_here = cols_here // tile
    flags = lax.dynamic_slice_in_dim(ancestors, col_index * tiles_here, tiles_here, 1)
    flags = jnp.where((start_order == 0)[:, None], flags[:1], flags[1:]) if sections == 2 else flags[start_order]
    col_masks = jnp.repeat(flags.astype(jnp.float32), tile, axis=1)

    turns = jnp.arange(steps)
    outers = jnp.stack([(outer - 1 - turns) % steps, (outer + 1 + turns) % steps])
    rows_wanted = outers[:, :, None] * INNER + jnp.stack([1 - inner, inner])[None, None, :]
    table = ((rows_wanted // ratio) ^ col_index) * ratio + rows_wanted % ratio
    table = table.reshape(2, steps * INNER).astype(jnp.int32)

    forward = [(r, (r + INNER) % row_count) for r in range(row_count)]
    backward = [(b, a) for a, b in forward]
    across = [(r, r ^ 1) for r in range(row_count)]

    gathered = [gather_pieces(own[s : s + 1]) for s in range(sections)]

    row_results, col_results, diag_parts = [], [], []
    for s, pieces in enumerate(gathered):
        sends, kept = panel_terms(table, resident_inverse, pieces, ratio)
        carry = [None, None]
        for step in range(steps):
            arrived = lax.ppermute(sends[step], "row", across)
            for h in range(2):
                here = kept[step, :, h] + arrived[:, h]
                if step:
                    ring = forward if h == 0 else backward
                    here = here + lax.ppermute(carry[h], "row", ring)
                carry[h] = here
        masks = col_masks[s : s + 1, None, :]
        finished = [-carry[h] * masks[:, :, h * half : (h + 1) * half] for h in range(2)]
        if ratio == 2:
            turned = mirrored(finished)
        else:
            joined = jnp.concatenate(finished, axis=-1)
            turned = mirrored([joined[:, :, q * rows_here : (q + 1) * rows_here] for q in range(ratio)])
        row_results.append(jnp.concatenate(finished, axis=-1))
        column = unmirror(turned, 1)
        col_results.append(column)
        diag_parts.append(diag_terms(column, pieces))

    rest = jnp.concatenate(diag_parts, axis=0).reshape(sections, row_count, narrow, slice_width)
    place = ((row_index // ratio) ^ col_index) * ratio + row_index % ratio
    for bit in range(row_count.bit_length() - 1):
        own_bit = (place >> bit) & 1
        shaped = rest.reshape(sections, -1, 2, narrow, slice_width)
        outgoing = lax.dynamic_index_in_dim(shaped, 1 - own_bit, 2, keepdims=False)
        stays = lax.dynamic_index_in_dim(shaped, own_bit, 2, keepdims=False)
        rest = stays + swap_bit(outgoing, "row", bit)
    if sections == 2:
        flipped = jnp.flip(diag_inverse, axis=0)
        sectioned_diag = jnp.where(start_order[0] == 0, diag_inverse, flipped)
    else:
        sectioned_diag = jnp.take(diag_inverse, start_order, axis=0)
    diag_result = sectioned_diag - rest.reshape(sections, narrow, slice_width)

    col_out = jnp.swapaxes(jnp.concatenate(col_results, axis=0), 1, 2)
    return (col_out, jnp.concatenate(row_results, axis=0), diag_result)


def solution(mesh):
    return jax.shard_map(
        on_device,
        mesh=mesh,
        in_specs=(P("row", "col"), P(None, "row", "col"), P(None, "row", "col"), P(), P()),
        out_specs=(P(None, "row", "col"), P(None, "row", "col"), P(None, "row", "col")),
        check_vma=False,
    )
```

profile of v0, /device:TPU:0, one launch (start us, length us, event | category | flops | bytes accessed | tf_op | source)
XLA Modules:
  0.0 180.6 jit_solution(10485953733277055732)
XLA Ops:
  3.8 3.1 %collective-permute-start.1 = (f32[1,64,1536]{2,1,0:T(8,128)S(1)}, f32[1,64,1536]{2,1,0:T(8,128)S(1)}, u32[]{:S(2)}, u32[]{:S(2)}) collective-permute-start(f32[1,64,1536]{2,1,0:T(8,128)S(1)} %get-tuple-element.45.refs_0_), channel_id=1, source_target_pairs={{0,2},{1,3},{2,0},{3,1},{4,6},{5,7},{6,4},{7,5},{8,10},{9,11},{10,... | collective-permute-start | bytes 1179656 | tf_op jit(solution)/shard_map/ppermute | solution.py:14
  7.8 9.1 %collective-permute-done.1.refs_2_ = f32[1,64,1536]{2,1,0:T(8,128)S(1)} collective-permute-done((f32[1,64,1536]{2,1,0:T(8,128)S(1)}, f32[1,64,1536]{2,1,0:T(8,128)S(1)}, u32[]{:S(2)}, u32[]{:S(2)}) %collective-permute-start.1) | collective-permute-done | bytes 393248 | tf_op jit(solution)/shard_map/ppermute | solution.py:14
  17.4 7.1 %collective-permute-done.18.refs_2_ = f32[1,64,1536]{2,1,0:T(8,128)S(1)} collective-permute-done((f32[1,64,1536]{2,1,0:T(8,128)S(1)}, f32[1,64,1536]{2,1,0:T(8,128)S(1)}, u32[]{:S(2)}, u32[]{:S(2)}) %collective-permute-start.18) | collective-permute-done | bytes 393248 | tf_op jit(solution)/shard_map/ppermute | solution.py:14
  24.5 12.7 %panel_terms.2 = (f32[1,2,32,1536]{3,2,1,0:T(8,128)S(1)}, f32[1,2,32,1536]{3,2,1,0:T(8,128)S(1)}, f32[1,2,32,1536]{3,2,1,0:T(8,128)S(1)}, f32[1,2,32,1536]{3,2,1,0:T(8,128)S(1)}, f32[4,1,2,32,1536]{4,3,2,1,0:T(8,128)S(1)}) custom-call(s32[2,8]{1,0:T(2,128)S(1)} %fusion.37.table_ref, f32[1536,3072]{1,0:T(8,128)} %inverse_ref.3, ...), custom_call_target="tpu_custom_call" | custom-call | flops 7247757312 | bytes 18874368 | tf_op jit(solution)/shard_map/panel_terms/pallas_call | solution.py:103
  41.2 12.6 %panel_terms.3 = (f32[1,2,32,1536]{3,2,1,0:T(8,128)S(1)}, f32[1,2,32,1536]{3,2,1,0:T(8,128)S(1)}, f32[1,2,32,1536]{3,2,1,0:T(8,128)S(1)}, f32[1,2,32,1536]{3,2,1,0:T(8,128)S(1)}, f32[4,1,2,32,1536]{4,3,2,1,0:T(8,128)S(1)}) custom-call(s32[2,8]{1,0:T(2,128)S(1)} %fusion.37.table_ref, f32[1536,3072]{1,0:T(8,128)} %inverse_ref.3, ...), custom_call_target="tpu_custom_call" | custom-call | flops 7247757312 | bytes 18874368 | tf_op jit(solution)/shard_map/panel_terms/pallas_call | solution.py:103
  55.7 3.7 %collective-permute-start.10 = (f32[1,32,1536]{2,1,0:T(8,128)S(1)}, f32[1,32,1536]{2,1,0:T(8,128)S(1)}, u32[]{:S(2)}, u32[]{:S(2)}) collective-permute-start(f32[1,32,1536]{2,1,0:T(8,128)S(1)} %get-tuple-element.37), channel_id=1, source_target_pairs={{8,0},{12,4},{16,8},{20,12},{24,16},{28,20},{0,24},{4,28},{9,1},{1... | collective-permute-start | bytes 589832 | tf_op jit(solution)/shard_map/ppermute | solution.py:258
  59.4 23.0 %collective-permute-done.23 = f32[1,2,32,1536]{3,2,1,0:T(8,128)S(1)} collective-permute-done((f32[1,2,32,1536]{3,2,1,0:T(8,128)S(1)}, f32[1,2,32,1536]{3,2,1,0:T(8,128)S(1)}, u32[]{:S(2)}, u32[]{:S(2)}) %collective-permute-start.23) | collective-permute-done | bytes 393248 | tf_op jit(solution)/shard_map/ppermute | solution.py:253
  87.4 4.6 %collective-permute-done.7 = f32[1,32,1536]{2,1,0:T(8,128)S(1)} collective-permute-done((f32[1,32,1536]{2,1,0:T(8,128)S(1)}, f32[1,32,1536]{2,1,0:T(8,128)S(1)}, u32[]{:S(2)}, u32[]{:S(2)}) %collective-permute-start.7) | collective-permute-done | bytes 196640 | tf_op jit(solution)/shard_map/ppermute | solution.py:258
  96.2 2.8 %collective-permute-start.11 = (f32[1,32,1536]{2,1,0:T(8,128)S(1)}, f32[1,32,1536]{2,1,0:T(8,128)S(1)}, u32[]{:S(2)}, u32[]{:S(2)}) collective-permute-start(f32[1,32,1536]{2,1,0:T(8,128)S(1)} %get-tuple-element.35), channel_id=1, source_target_pairs={{8,0},{12,4},{16,8},{20,12},{24,16},{28,20},{0,24},{4,28},{9,1},{1... | collective-permute-start | bytes 589832 | tf_op jit(solution)/shard_map/ppermute | solution.py:258
  102.1 2.1 %collective-permute-done.11 = f32[1,32,1536]{2,1,0:T(8,128)S(1)} collective-permute-done((f32[1,32,1536]{2,1,0:T(8,128)S(1)}, f32[1,32,1536]{2,1,0:T(8,128)S(1)}, u32[]{:S(2)}, u32[]{:S(2)}) %collective-permute-start.11) | collective-permute-done | bytes 196640 | tf_op jit(solution)/shard_map/ppermute | solution.py:258
  104.4 4.3 %collective-permute-done.8 = f32[1,32,1536]{2,1,0:T(8,128)S(1)} collective-permute-done((f32[1,32,1536]{2,1,0:T(8,128)S(1)}, f32[1,32,1536]{2,1,0:T(8,128)S(1)}, u32[]{:S(2)}, u32[]{:S(2)}) %collective-permute-start.8) | collective-permute-done | bytes 196640 | tf_op jit(solution)/shard_map/ppermute | solution.py:258
  108.7 2.4 %collective-permute-start.28 = (f32[1,32,1536]{2,1,0:T(8,128)S(1)}, f32[1,32,1536]{2,1,0:T(8,128)S(1)}, u32[]{:S(2)}, u32[]{:S(2)}) collective-permute-start(f32[1,32,1536]{2,1,0:T(8,128)S(1)} %get-tuple-element.41), channel_id=1, source_target_pairs={{8,0},{12,4},{16,8},{20,12},{24,16},{28,20},{0,24},{4,28},{9,1},{1... | collective-permute-start | bytes 589832 | tf_op jit(solution)/shard_map/ppermute | solution.py:258
  111.6 2.7 %collective-permute-done.25 = f32[1,32,1536]{2,1,0:T(8,128)S(1)} collective-permute-done((f32[1,32,1536]{2,1,0:T(8,128)S(1)}, f32[1,32,1536]{2,1,0:T(8,128)S(1)}, u32[]{:S(2)}, u32[]{:S(2)}) %collective-permute-start.25) | collective-permute-done | bytes 196640 | tf_op jit(solution)/shard_map/ppermute | solution.py:258
  114.3 3.2 %collective-permute-done.28 = f32[1,32,1536]{2,1,0:T(8,128)S(1)} collective-permute-done((f32[1,32,1536]{2,1,0:T(8,128)S(1)}, f32[1,32,1536]{2,1,0:T(8,128)S(1)}, u32[]{:S(2)}, u32[]{:S(2)}) %collective-permute-start.28) | collective-permute-done | bytes 196640 | tf_op jit(solution)/shard_map/ppermute | solution.py:258
  118.9 2.6 %collective-permute-start.29 = (f32[1,32,1536]{2,1,0:T(8,128)S(1)}, f32[1,32,1536]{2,1,0:T(8,128)S(1)}, u32[]{:S(2)}, u32[]{:S(2)}) collective-permute-start(f32[1,32,1536]{2,1,0:T(8,128)S(1)} %get-tuple-element.39), channel_id=1, source_target_pairs={{8,0},{12,4},{16,8},{20,12},{24,16},{28,20},{0,24},{4,28},{9,1},{1... | collective-permute-start | bytes 589832 | tf_op jit(solution)/shard_map/ppermute | solution.py:258
  121.5 7.6 %collective-permute-done.12 = f32[1,32,1536]{2,1,0:T(8,128)S(1)} collective-permute-done((f32[1,32,1536]{2,1,0:T(8,128)S(1)}, f32[1,32,1536]{2,1,0:T(8,128)S(1)}, u32[]{:S(2)}, u32[]{:S(2)}) %collective-permute-start.12) | collective-permute-done | bytes 196640 | tf_op jit(solution)/shard_map/ppermute | solution.py:258
  130.5 3.2 %collective-permute-start.13 = (f32[1,32,1536]{2,1,0:T(8,128)S(1)}, f32[1,32,1536]{2,1,0:T(8,128)S(1)}, u32[]{:S(2)}, u32[]{:S(2)}) collective-permute-start(f32[1,32,1536]{2,1,0:T(8,128)S(1)} %get-tuple-element.27), channel_id=1, source_target_pairs={{0,4},{1,12},{4,0},{5,8},{8,5},{9,13},{12,1},{13,9},{18,22},{19,30... | collective-permute-start | bytes 589832 | tf_op jit(solution)/shard_map/ppermute | solution.py:165
  135.1 2.9 %collective-permute-start.30 = (f32[1,32,1536]{2,1,0:T(8,128)S(1)}, f32[1,32,1536]{2,1,0:T(8,128)S(1)}, u32[]{:S(2)}, u32[]{:S(2)}) collective-permute-start(f32[1,32,1536]{2,1,0:T(8,128)S(1)} %get-tuple-element.30), channel_id=1, source_target_pairs={{0,4},{1,12},{4,0},{5,8},{8,5},{9,13},{12,1},{13,9},{18,22},{19,30... | collective-permute-start | bytes 589832 | tf_op jit(solution)/shard_map/ppermute | solution.py:165
  138.7 6.4 %collective-permute-start.15 = (f32[1,32,1536]{2,1,0:T(8,128)S(1)}, f32[1,32,1536]{2,1,0:T(8,128)S(1)}, u32[]{:S(2)}, u32[]{:S(2)}) collective-permute-start(f32[1,32,1536]{2,1,0:T(8,128)S(1)} %collective-permute-done.14), channel_id=1, source_target_pairs={{0,20},{1,28},{4,16},{5,24},{8,21},{9,29},{12,17},{13,25},{18,6},{... | collective-permute-start | bytes 589832 | tf_op jit(solution)/shard_map/ppermute | solution.py:168
  145.8 14.2 %collective-permute-start.32 = (f32[1,32,1536]{2,1,0:T(8,128)S(1)}, f32[1,32,1536]{2,1,0:T(8,128)S(1)}, u32[]{:S(2)}, u32[]{:S(2)}) collective-permute-start(f32[1,32,1536]{2,1,0:T(8,128)S(1)} %collective-permute-done.31), channel_id=1, source_target_pairs={{0,20},{1,28},{4,16},{5,24},{8,21},{9,29},{12,17},{13,25},{18,6},{... | collective-permute-start | bytes 589832 | tf_op jit(solution)/shard_map/ppermute | solution.py:168
  160.1 3.0 %collective-permute-done.32 = f32[1,32,1536]{2,1,0:T(8,128)S(1)} collective-permute-done((f32[1,32,1536]{2,1,0:T(8,128)S(1)}, f32[1,32,1536]{2,1,0:T(8,128)S(1)}, u32[]{:S(2)}, u32[]{:S(2)}) %collective-permute-start.32) | collective-permute-done | bytes 196640 | tf_op jit(solution)/shard_map/ppermute | solution.py:168
  165.8 4.1 %collective-permute-done.34 = f32[2,4,32,64]{3,2,1,0:T(8,128)S(1)} collective-permute-done((f32[2,4,32,64]{3,2,1,0:T(8,128)S(1)}, f32[2,4,32,64]{3,2,1,0:T(8,128)S(1)}, u32[]{:S(2)}, u32[]{:S(2)}) %collective-permute-start.34) | collective-permute-done | bytes 65568 | tf_op jit(solution)/shard_map/ppermute | solution.py:14
  171.0 3.6 %collective-permute-done.35 = f32[2,2,32,64]{3,2,1,0:T(8,128)S(1)} collective-permute-done((f32[2,2,32,64]{3,2,1,0:T(8,128)S(1)}, f32[2,2,32,64]{3,2,1,0:T(8,128)S(1)}, u32[]{:S(2)}, u32[]{:S(2)}) %collective-permute-start.35) | collective-permute-done | bytes 32800 | tf_op jit(solution)/shard_map/ppermute | solution.py:14
  174.7 3.4 %collective-permute-start.36 = (f32[2,1,32,64]{3,2,1,0:T(8,128)S(1)}, f32[2,1,32,64]{3,2,1,0:T(8,128)S(1)}, u32[]{:S(2)}, u32[]{:S(2)}) collective-permute-start(f32[2,1,32,64]{3,2,1,0:T(8,128)S(1)} %constant_dynamic-slice_fusion), channel_id=1, source_target_pairs={{0,16},{4,20},{8,24},{12,28},{16,0},{20,4},{24,8},{28,12},{1,17},{... | collective-permute-start | bytes 49160 | tf_op jit(solution)/shard_map/ppermute | solution.py:14
  (126 shorter events, 35.1 us)
Async XLA Ops:
  3.8 13.0 %collective-permute-start.1 = (f32[1,64,1536]{2,1,0:T(8,128)S(1)}, f32[1,64,1536]{2,1,0:T(8,128)S(1)}, u32[]{:S(2)}, u32[]{:S(2)}) collective-permute-start(f32[1,64,1536]{2,1,0:T(8,128)S(1)} %get-tuple-element.45.refs_0_), channel_id=1, source_target_pairs={{0,2},{1,3},{2,0},{3,1},{4,6},{5,7},{6,4},{7,5},{8,10},{9,11},{10,... | collective-permute-start | bytes 1179656 | tf_op jit(solution)/shard_map/ppermute | solution.py:14
  6.9 17.5 %collective-permute-start = (f32[1,64,1536]{2,1,0:T(8,128)S(1)}, f32[1,64,1536]{2,1,0:T(8,128)S(1)}, u32[]{:S(2)}, u32[]{:S(2)}) collective-permute-start(f32[1,64,1536]{2,1,0:T(8,128)S(1)} %get-tuple-element.45.refs_0_), channel_id=1, source_target_pairs={{0,1},{1,0},{2,3},{3,2},{4,5},{5,4},{6,7},{7,6},{8,9},{9,8},{10,11... | collective-permute-start | bytes 1179656 | tf_op jit(solution)/shard_map/ppermute | solution.py:14
  6.9 17.5 %collective-permute-start.18 = (f32[1,64,1536]{2,1,0:T(8,128)S(1)}, f32[1,64,1536]{2,1,0:T(8,128)S(1)}, u32[]{:S(2)}, u32[]{:S(2)}) collective-permute-start(f32[1,64,1536]{2,1,0:T(8,128)S(1)} %get-tuple-element.46.refs_0_), channel_id=1, source_target_pairs={{0,2},{1,3},{2,0},{3,1},{4,6},{5,7},{6,4},{7,5},{8,10},{9,11},{10,... | collective-permute-start | bytes 1179656 | tf_op jit(solution)/shard_map/ppermute | solution.py:14
  7.1 33.9 %collective-permute-start.17 = (f32[1,64,1536]{2,1,0:T(8,128)S(1)}, f32[1,64,1536]{2,1,0:T(8,128)S(1)}, u32[]{:S(2)}, u32[]{:S(2)}) collective-permute-start(f32[1,64,1536]{2,1,0:T(8,128)S(1)} %get-tuple-element.46.refs_0_), channel_id=1, source_target_pairs={{0,1},{1,0},{2,3},{3,2},{4,5},{5,4},{6,7},{7,6},{8,9},{9,8},{10,11... | collective-permute-start | bytes 1179656 | tf_op jit(solution)/shard_map/ppermute | solution.py:14
  24.4 16.8 %collective-permute-start.19 = (f32[1,64,1536]{2,1,0:T(8,128)S(1)}, f32[1,64,1536]{2,1,0:T(8,128)S(1)}, u32[]{:S(2)}, u32[]{:S(2)}) collective-permute-start(f32[1,64,1536]{2,1,0:T(8,128)S(1)} %collective-permute-done.18.refs_2_), channel_id=1, source_target_pairs={{0,1},{1,0},{2,3},{3,2},{4,5},{5,4},{6,7},{7,6},{8,9},{9,8},{10,11... | collective-permute-start | bytes 1179656 | tf_op jit(solution)/shard_map/ppermute | solution.py:14
  37.1 18.6 %collective-permute-start.6 = (f32[1,2,32,1536]{3,2,1,0:T(8,128)S(1)}, f32[1,2,32,1536]{3,2,1,0:T(8,128)S(1)}, u32[]{:S(2)}, u32[]{:S(2)}) collective-permute-start(f32[1,2,32,1536]{3,2,1,0:T(8,128)S(1)} %get-tuple-element.17), channel_id=1, source_target_pairs={{0,4},{4,0},{8,12},{12,8},{16,20},{20,16},{24,28},{28,24},{1,5},{5... | collective-permute-start | bytes 1179656 | tf_op jit(solution)/shard_map/ppermute | solution.py:253
  38.9 45.4 %collective-permute-start.5 = (f32[1,2,32,1536]{3,2,1,0:T(8,128)S(1)}, f32[1,2,32,1536]{3,2,1,0:T(8,128)S(1)}, u32[]{:S(2)}, u32[]{:S(2)}) collective-permute-start(f32[1,2,32,1536]{3,2,1,0:T(8,128)S(1)} %get-tuple-element.16), channel_id=1, source_target_pairs={{0,4},{4,0},{8,12},{12,8},{16,20},{20,16},{24,28},{28,24},{1,5},{5... | collective-permute-start | bytes 1179656 | tf_op jit(solution)/shard_map/ppermute | solution.py:253
  39.2 61.3 %collective-permute-start.4 = (f32[1,2,32,1536]{3,2,1,0:T(8,128)S(1)}, f32[1,2,32,1536]{3,2,1,0:T(8,128)S(1)}, u32[]{:S(2)}, u32[]{:S(2)}) collective-permute-start(f32[1,2,32,1536]{3,2,1,0:T(8,128)S(1)} %get-tuple-element.15), channel_id=1, source_target_pairs={{0,4},{4,0},{8,12},{12,8},{16,20},{20,16},{24,28},{28,24},{1,5},{5... | collective-permute-start | bytes 1179656 | tf_op jit(solution)/shard_map/ppermute | solution.py:253
  40.9 77.9 %collective-permute-start.3 = (f32[1,2,32,1536]{3,2,1,0:T(8,128)S(1)}, f32[1,2,32,1536]{3,2,1,0:T(8,128)S(1)}, u32[]{:S(2)}, u32[]{:S(2)}) collective-permute-start(f32[1,2,32,1536]{3,2,1,0:T(8,128)S(1)} %get-tuple-element.14), channel_id=1, source_target_pairs={{0,4},{4,0},{8,12},{12,8},{16,20},{20,16},{24,28},{28,24},{1,5},{5... | collective-permute-start | bytes 1179656 | tf_op jit(solution)/shard_map/ppermute | solution.py:253
  53.9 28.5 %collective-permute-start.23 = (f32[1,2,32,1536]{3,2,1,0:T(8,128)S(1)}, f32[1,2,32,1536]{3,2,1,0:T(8,128)S(1)}, u32[]{:S(2)}, u32[]{:S(2)}) collective-permute-start(f32[1,2,32,1536]{3,2,1,0:T(8,128)S(1)} %get-tuple-element.22), channel_id=1, source_target_pairs={{0,4},{4,0},{8,12},{12,8},{16,20},{20,16},{24,28},{28,24},{1,5},{5... | collective-permute-start | bytes 1179656 | tf_op jit(solution)/shard_map/ppermute | solution.py:253
  55.7 30.1 %collective-permute-start.10 = (f32[1,32,1536]{2,1,0:T(8,128)S(1)}, f32[1,32,1536]{2,1,0:T(8,128)S(1)}, u32[]{:S(2)}, u32[]{:S(2)}) collective-permute-start(f32[1,32,1536]{2,1,0:T(8,128)S(1)} %get-tuple-element.37), channel_id=1, source_target_pairs={{8,0},{12,4},{16,8},{20,12},{24,16},{28,20},{0,24},{4,28},{9,1},{1... | collective-permute-start | bytes 589832 | tf_op jit(solution)/shard_map/ppermute | solution.py:258
  84.3 10.4 %collective-permute-start.22 = (f32[1,2,32,1536]{3,2,1,0:T(8,128)S(1)}, f32[1,2,32,1536]{3,2,1,0:T(8,128)S(1)}, u32[]{:S(2)}, u32[]{:S(2)}) collective-permute-start(f32[1,2,32,1536]{3,2,1,0:T(8,128)S(1)} %get-tuple-element.21), channel_id=1, source_target_pairs={{0,4},{4,0},{8,12},{12,8},{16,20},{20,16},{24,28},{28,24},{1,5},{5... | collective-permute-start | bytes 1179656 | tf_op jit(solution)/shard_map/ppermute | solution.py:253
  94.7 16.5 %collective-permute-start.21 = (f32[1,2,32,1536]{3,2,1,0:T(8,128)S(1)}, f32[1,2,32,1536]{3,2,1,0:T(8,128)S(1)}, u32[]{:S(2)}, u32[]{:S(2)}) collective-permute-start(f32[1,2,32,1536]{3,2,1,0:T(8,128)S(1)} %get-tuple-element.20), channel_id=1, source_target_pairs={{0,4},{4,0},{8,12},{12,8},{16,20},{20,16},{24,28},{28,24},{1,5},{5... | collective-permute-start | bytes 1179656 | tf_op jit(solution)/shard_map/ppermute | solution.py:253
  100.5 33.2 %collective-permute-start.20 = (f32[1,2,32,1536]{3,2,1,0:T(8,128)S(1)}, f32[1,2,32,1536]{3,2,1,0:T(8,128)S(1)}, u32[]{:S(2)}, u32[]{:S(2)}) collective-permute-start(f32[1,2,32,1536]{3,2,1,0:T(8,128)S(1)} %get-tuple-element.19), channel_id=1, source_target_pairs={{0,4},{4,0},{8,12},{12,8},{16,20},{20,16},{24,28},{28,24},{1,5},{5... | collective-permute-start | bytes 1179656 | tf_op jit(solution)/shard_map/ppermute | solution.py:253
  111.3 17.8 %collective-permute-start.12 = (f32[1,32,1536]{2,1,0:T(8,128)S(1)}, f32[1,32,1536]{2,1,0:T(8,128)S(1)}, u32[]{:S(2)}, u32[]{:S(2)}) collective-permute-start(f32[1,32,1536]{2,1,0:T(8,128)S(1)} %get-tuple-element.33), channel_id=1, source_target_pairs={{8,0},{12,4},{16,8},{20,12},{24,16},{28,20},{0,24},{4,28},{9,1},{1... | collective-permute-start | bytes 589832 | tf_op jit(solution)/shard_map/ppermute | solution.py:258
  114.3 14.8 %collective-permute-start.9 = (f32[1,32,1536]{2,1,0:T(8,128)S(1)}, f32[1,32,1536]{2,1,0:T(8,128)S(1)}, u32[]{:S(2)}, u32[]{:S(2)}) collective-permute-start(f32[1,32,1536]{2,1,0:T(8,128)S(1)} %get-tuple-element.34), channel_id=1, source_target_pairs={{0,8},{4,12},{8,16},{12,20},{16,24},{20,28},{24,0},{28,4},{1,9},{5... | collective-permute-start | bytes 589832 | tf_op jit(solution)/shard_map/ppermute | solution.py:258
  117.6 16.1 %collective-permute-start.26 = (f32[1,32,1536]{2,1,0:T(8,128)S(1)}, f32[1,32,1536]{2,1,0:T(8,128)S(1)}, u32[]{:S(2)}, u32[]{:S(2)}) collective-permute-start(f32[1,32,1536]{2,1,0:T(8,128)S(1)} %get-tuple-element.40), channel_id=1, source_target_pairs={{0,8},{4,12},{8,16},{12,20},{16,24},{20,28},{24,0},{28,4},{1,9},{5... | collective-permute-start | bytes 589832 | tf_op jit(solution)/shard_map/ppermute | solution.py:258
  118.9 14.8 %collective-permute-start.29 = (f32[1,32,1536]{2,1,0:T(8,128)S(1)}, f32[1,32,1536]{2,1,0:T(8,128)S(1)}, u32[]{:S(2)}, u32[]{:S(2)}) collective-permute-start(f32[1,32,1536]{2,1,0:T(8,128)S(1)} %get-tuple-element.39), channel_id=1, source_target_pairs={{8,0},{12,4},{16,8},{20,12},{24,16},{28,20},{0,24},{4,28},{9,1},{1... | collective-permute-start | bytes 589832 | tf_op jit(solution)/shard_map/ppermute | solution.py:258
  130.5 29.5 %collective-permute-start.13 = (f32[1,32,1536]{2,1,0:T(8,128)S(1)}, f32[1,32,1536]{2,1,0:T(8,128)S(1)}, u32[]{:S(2)}, u32[]{:S(2)}) collective-permute-start(f32[1,32,1536]{2,1,0:T(8,128)S(1)} %get-tuple-element.27), channel_id=1, source_target_pairs={{0,4},{1,12},{4,0},{5,8},{8,5},{9,13},{12,1},{13,9},{18,22},{19,30... | collective-permute-start | bytes 589832 | tf_op jit(solution)/shard_map/ppermute | solution.py:165
  133.8 12.0 %collective-permute-start.31 = (f32[1,32,1536]{2,1,0:T(8,128)S(1)}, f32[1,32,1536]{2,1,0:T(8,128)S(1)}, u32[]{:S(2)}, u32[]{:S(2)}) collective-permute-start(f32[1,32,1536]{2,1,0:T(8,128)S(1)} %get-tuple-element.30), channel_id=1, source_target_pairs={{2,0},{3,1},{6,4},{7,5},{10,8},{11,9},{14,12},{15,13},{16,18},{17,... | collective-permute-start | bytes 589832 | tf_op jit(solution)/shard_map/ppermute | solution.py:167
  135.1 25.0 %collective-permute-start.30 = (f32[1,32,1536]{2,1,0:T(8,128)S(1)}, f32[1,32,1536]{2,1,0:T(8,128)S(1)}, u32[]{:S(2)}, u32[]{:S(2)}) collective-permute-start(f32[1,32,1536]{2,1,0:T(8,128)S(1)} %get-tuple-element.30), channel_id=1, source_target_pairs={{0,4},{1,12},{4,0},{5,8},{8,5},{9,13},{12,1},{13,9},{18,22},{19,30... | collective-permute-start | bytes 589832 | tf_op jit(solution)/shard_map/ppermute | solution.py:165
  138.7 21.3 %collective-permute-start.15 = (f32[1,32,1536]{2,1,0:T(8,128)S(1)}, f32[1,32,1536]{2,1,0:T(8,128)S(1)}, u32[]{:S(2)}, u32[]{:S(2)}) collective-permute-start(f32[1,32,1536]{2,1,0:T(8,128)S(1)} %collective-permute-done.14), channel_id=1, source_target_pairs={{0,20},{1,28},{4,16},{5,24},{8,21},{9,29},{12,17},{13,25},{18,6},{... | collective-permute-start | bytes 589832 | tf_op jit(solution)/shard_map/ppermute | solution.py:168
  145.1 15.0 %collective-permute-start.33 = (f32[1,32,1536]{2,1,0:T(8,128)S(1)}, f32[1,32,1536]{2,1,0:T(8,128)S(1)}, u32[]{:S(2)}, u32[]{:S(2)}) collective-permute-start(f32[1,32,1536]{2,1,0:T(8,128)S(1)} %broadcast_select_fusion.2), channel_id=1, source_target_pairs={{0,0},{1,8},{2,16},{3,24},{4,4},{5,12},{6,20},{7,28},{8,1},{9,9},{... | collective-permute-start | bytes 589832 | tf_op jit(solution)/shard_map/ppermute | solution.py:165
  145.8 17.3 %collective-permute-start.32 = (f32[1,32,1536]{2,1,0:T(8,128)S(1)}, f32[1,32,1536]{2,1,0:T(8,128)S(1)}, u32[]{:S(2)}, u32[]{:S(2)}) collective-permute-start(f32[1,32,1536]{2,1,0:T(8,128)S(1)} %collective-permute-done.31), channel_id=1, source_target_pairs={{0,20},{1,28},{4,16},{5,24},{8,21},{9,29},{12,17},{13,25},{18,6},{... | collective-permute-start | bytes 589832 | tf_op jit(solution)/shard_map/ppermute | solution.py:168
  (27 other events, 268.7 us)
where the time goes:
time: 181 us
  waiting for transfers between devices  77.4 us (43%)
  starting transfers between devices  67.9 us (38%)
  Pallas kernels  27.4 us (15%)
  other arithmetic  3.5 us (2%)
  local copies, waits for them, and re-layouts  3.2 us (2%)
    ppermute x12, waiting for transfers between devices, on_device(): here = here + lax.ppermute(carry[h], 'row', ring)  25.8 us
    pallas_call x2, Pallas kernels, panel_terms(): pl.pallas_call(functools.partial(terms_kernel, (count, ratio, narrow, ste...  25.3 us
    ppermute x9, waiting for transfers between devices, swap_bit(): return lax.ppermute(block, axis, [(i, i ^ 1 << bit) for i in range(count)])  24.8 us
    ppermute x8, waiting for transfers between devices, on_device(): arrived = lax.ppermute(sends[step], 'row', across)  23.7 us
    ppermute x2, starting transfers between devices, mirrored(): got = got + lax.ppermute(halfway, ('row', 'col'), second)  20.5 us
    ppermute x12, starting transfers between devices, on_device(): here = here + lax.ppermute(carry[h], 'row', ring)  18.8 us
    ppermute x8, starting transfers between devices, on_device(): arrived = lax.ppermute(sends[step], 'row', across)  10.6 us
    ppermute x9, starting transfers between devices, swap_bit(): return lax.ppermute(block, axis, [(i, i ^ 1 << bit) for i in range(count)])  8.03 us
  transfers between devices with their start and end apart: 37, of which 15 were waited for; matrix products, arithmetic and copies ran while one was open for 2% of the time, Pallas kernels for 14%

commit v1 on v0

--- a/solution.py
+++ b/solution.py
@@ -1,4 +1,5 @@
 import functools
+import math
 import jax
 import jax.numpy as jnp
 from jax import lax
@@ -23,37 +24,12 @@
     return lax.dot_general(left, right, (contract, ((), ())), preferred_element_type=jnp.float32)
 
 
-def mask_kernel(tile, order_ref, flags_ref, place_ref, panel_ref, out_ref):
-    section = order_ref[pl.program_id(0)]
-    for t in range(panel_ref.shape[2] // tile):
-        flag = flags_ref[section, place_ref[0] + t].astype(jnp.float32)
-        at = pl.ds(t * tile, tile)
-        out_ref[0, :, at] = panel_ref[0, :, at] * flag
-
-
-def masked_panels(panel, ancestors, start_order, first_tile, tile):
-    sections, width, rows = panel.shape
-    return pl.pallas_call(
-        functools.partial(mask_kernel, tile),
-        grid_spec=pltpu.PrefetchScalarGridSpec(
-            num_scalar_prefetch=3,
-            grid=(sections,),
-            in_specs=[pl.BlockSpec((1, width, rows), lambda s, order, flags, place: (order[s], 0, 0))],
-            out_specs=pl.BlockSpec((1, width, rows), lambda s, order, flags, place: (s, 0, 0)),
-        ),
-        out_shape=jax.ShapeDtypeStruct(panel.shape, jnp.float32),
-        compiler_params=pltpu.CompilerParams(vmem_limit_bytes=8 << 20),
-        cost_estimate=pl.CostEstimate(flops=panel.size, bytes_accessed=8 * panel.size, transcendentals=0),
-        name="mask_panels",
-    )(start_order, ancestors, first_tile, panel)
-
-
 def column_block(columns):
     return next(columns // t for t in range(1, columns + 1) if columns % t == 0 and columns // t <= 512)
 
 
-def terms_kernel(dims, table_ref, inverse_ref, *refs):
-    pieces_count, ratio, narrow, steps, members = dims
+def terms_kernel(dims, table_ref, flags_ref, place_ref, inverse_ref, *refs):
+    pieces_count, ratio, narrow, steps, members, node, tile = dims
     pieces, refs = refs[:pieces_count], refs[pieces_count:]
     sends, (kept_ref, high_ref, low_ref, left_ref) = refs[:steps], refs[steps:]
     h = pl.program_id(0)
@@ -64,10 +40,13 @@
     def _():
         for m in range(pieces_count):
             for g in range(members):
-                for l in range(ratio):
-                    high, low = split(pieces[m][g, l * narrow : (l + 1) * narrow, :])
-                    high_ref[m * ratio + l, g] = high
-                    low_ref[m * ratio + l, g] = low
+                for t in range(left_ref.shape[1] // tile):
+                    at = slice(t * tile, (t + 1) * tile)
+                    flag = flags_ref[node + g, place_ref[0] + t].astype(jnp.float32)
+                    for l in range(ratio):
+                        high, low = split(pieces[m][g, l * narrow : (l + 1) * narrow, at] * flag)
+                        high_ref[m * ratio + l, g, :, at] = high
+                        low_ref[m * ratio + l, g, :, at] = low
 
     @pl.when(n == 0)
     def _():
@@ -82,14 +61,19 @@
     high, low = split(inverse_ref[...])
     both = dot(left_ref[...], high, ((1,), (0,)))
     total = both[:rows] + both[rows:] + dot(left_ref[:rows, :], low, ((1,), (0,)))
-    total = total.reshape(members, steps, INNER, narrow, total.shape[1])
+    columns = total.shape[1]
+    chunk = math.gcd(columns, tile)
+    start = (h * pl.num_programs(1) + n) * columns
+    total = total.reshape(members, steps, INNER, narrow, columns)
     for g in range(members):
-        for j in range(steps):
-            sends[j][g, 0] = total[g, j, 0]
-            kept_ref[j, g, 0] = total[g, j, 1]
-
-
-def panel_terms(table, inverse, pieces, ratio):
+        for k in range(0, columns, chunk):
+            factor = -flags_ref[node + g, place_ref[1] + (start + k) // tile].astype(jnp.float32)
+            for j in range(steps):
+                sends[j][g, 0, :, k : k + chunk] = total[g, j, 0, :, k : k + chunk] * factor
+                kept_ref[j, g, 0, :, k : k + chunk] = total[g, j, 1, :, k : k + chunk] * factor
+
+
+def panel_terms(node, table, flags, place, inverse, pieces, ratio, tile):
     members, width, rows = pieces[0].shape
     count = len(pieces)
     steps = table.shape[1] // INNER
@@ -98,16 +82,16 @@
     block = column_block(half)
     tiles = half // block
     lefts = members * steps * INNER * narrow
-    whole = pl.BlockSpec((members, width, rows), lambda h, n, table: (0, 0, 0))
+    whole = pl.BlockSpec((members, width, rows), lambda h, n, table, flags, place: (0, 0, 0))
     flops = 6 * lefts * inverse.size
     outs = pl.pallas_call(
-        functools.partial(terms_kernel, (count, ratio, narrow, steps, members)),
+        functools.partial(terms_kernel, (count, ratio, narrow, steps, members, node, tile)),
         grid_spec=pltpu.PrefetchScalarGridSpec(
-            num_scalar_prefetch=1,
+            num_scalar_prefetch=3,
             grid=(2, tiles),
-            in_specs=[pl.BlockSpec((rows, block), lambda h, n, table: (0, h * tiles + n))] + [whole] * count,
-            out_specs=[pl.BlockSpec((members, 1, narrow, block), lambda h, n, table: (0, h, 0, n))] * steps
-            + [pl.BlockSpec((steps, members, 1, narrow, block), lambda h, n, table: (0, 0, h, 0, n))],
+            in_specs=[pl.BlockSpec((rows, block), lambda h, n, table, flags, place: (0, h * tiles + n))] + [whole] * count,
+            out_specs=[pl.BlockSpec((members, 1, narrow, block), lambda h, n, table, flags, place: (0, h, 0, n))] * steps
+            + [pl.BlockSpec((steps, members, 1, narrow, block), lambda h, n, table, flags, place: (0, 0, h, 0, n))],
             scratch_shapes=[
                 pltpu.VMEM((count * ratio, members, narrow, rows), jnp.bfloat16),
                 pltpu.VMEM((count * ratio, members, narrow, rows), jnp.bfloat16),
@@ -119,7 +103,7 @@
         compiler_params=pltpu.CompilerParams(vmem_limit_bytes=32 << 20),
         cost_estimate=pl.CostEstimate(flops=flops, bytes_accessed=4 * inverse.size, transcendentals=0),
         name="panel_terms",
-    )(table, inverse, *pieces)
+    )(table, flags, place, inverse, *pieces)
     return outs[:steps], outs[steps]
 
 
@@ -223,15 +207,9 @@
     steps = row_count // INNER
     outer = row_index // INNER
     inner = row_index % INNER
-    half = cols_here // 2
-
-    first_tile = (row_index * (rows_here // tile)).astype(jnp.int32).reshape(1)
-    own = masked_panels(jnp.swapaxes(factor_panel, 1, 2), ancestors, start_order, first_tile, tile)
-
-    tiles_here = cols_here // tile
-    flags = lax.dynamic_slice_in_dim(ancestors, col_index * tiles_here, tiles_here, 1)
-    flags = jnp.where((start_order == 0)[:, None], flags[:1], flags[1:]) if sections == 2 else flags[start_order]
-    col_masks = jnp.repeat(flags.astype(jnp.float32), tile, axis=1)
+
+    place = jnp.stack([row_index * (rows_here // tile), col_index * cols_here // tile]).astype(jnp.int32)
+    panel = jnp.swapaxes(factor_panel, 1, 2)
 
     turns = jnp.arange(steps)
     outers = jnp.stack([(outer - 1 - turns) % steps, (outer + 1 + turns) % steps])
@@ -243,11 +221,11 @@
     backward = [(b, a) for a, b in forward]
     across = [(r, r ^ 1) for r in range(row_count)]
 
-    gathered = [gather_pieces(own[s : s + 1]) for s in range(sections)]
+    gathered = [gather_pieces(panel[s : s + 1]) for s in range(sections)]
 
     row_results, col_results, diag_parts = [], [], []
     for s, pieces in enumerate(gathered):
-        sends, kept = panel_terms(table, resident_inverse, pieces, ratio)
+        sends, kept = panel_terms(s, table, ancestors, place, resident_inverse, pieces, ratio, tile)
         carry = [None, None]
         for step in range(steps):
             arrived = lax.ppermute(sends[step], "row", across)
@@ -257,8 +235,7 @@
                     ring = forward if h == 0 else backward
                     here = here + lax.ppermute(carry[h], "row", ring)
                 carry[h] = here
-        masks = col_masks[s : s + 1, None, :]
-        finished = [-carry[h] * masks[:, :, h * half : (h + 1) * half] for h in range(2)]
+        finished = carry
         if ratio == 2:
             turned = mirrored(finished)
         else:
@@ -270,22 +247,25 @@
         diag_parts.append(diag_terms(column, pieces))
 
     rest = jnp.concatenate(diag_parts, axis=0).reshape(sections, row_count, narrow, slice_width)
-    place = ((row_index // ratio) ^ col_index) * ratio + row_index % ratio
+    spot = ((row_index // ratio) ^ col_index) * ratio + row_index % ratio
     for bit in range(row_count.bit_length() - 1):
-        own_bit = (place >> bit) & 1
+        own_bit = (spot >> bit) & 1
         shaped = rest.reshape(sections, -1, 2, narrow, slice_width)
         outgoing = lax.dynamic_index_in_dim(shaped, 1 - own_bit, 2, keepdims=False)
         stays = lax.dynamic_index_in_dim(shaped, own_bit, 2, keepdims=False)
         rest = stays + swap_bit(outgoing, "row", bit)
-    if sections == 2:
-        flipped = jnp.flip(diag_inverse, axis=0)
-        sectioned_diag = jnp.where(start_order[0] == 0, diag_inverse, flipped)
-    else:
-        sectioned_diag = jnp.take(diag_inverse, start_order, axis=0)
-    diag_result = sectioned_diag - rest.reshape(sections, narrow, slice_width)
-
-    col_out = jnp.swapaxes(jnp.concatenate(col_results, axis=0), 1, 2)
-    return (col_out, jnp.concatenate(row_results, axis=0), diag_result)
+    diag_parts = list(diag_inverse - rest.reshape(sections, narrow, slice_width))
+    rows = [block[0] for block in row_results]
+    columns = [block[0] for block in col_results]
+    in_order = lambda blocks: sectioned(blocks, start_order)
+    return (jnp.swapaxes(in_order(columns), 1, 2), in_order(rows), in_order(diag_parts))
+
+
+def sectioned(blocks, order):
+    if len(blocks) == 2:
+        straight = order[0] == 0
+        return jnp.stack([jnp.where(straight, blocks[0], blocks[1]), jnp.where(straight, blocks[1], blocks[0])])
+    return jnp.take(jnp.stack(blocks), order, axis=0)
 
 
 def solution(mesh):

time: 181 us -> 179 us (0.989)
    unnamed x28 -> x6, local copies, waits for them, and re-layouts: 2.53 us -> 0.01 us
where the time goes in v1:
time: 179 us
  waiting for transfers between devices  77.6 us (43%)
  starting transfers between devices  67.9 us (38%)
  Pallas kernels  26.9 us (15%)
  other arithmetic  3.71 us (2%)
    ppermute x12, waiting for transfers between devices, on_device(): here = here + lax.ppermute(carry[h], 'row', ring)  25.8 us
    pallas_call x2, Pallas kernels, panel_terms(): pl.pallas_call(functools.partial(terms_kernel, (count, ratio, narrow, ste...  25.4 us
    ppermute x9, waiting for transfers between devices, swap_bit(): return lax.ppermute(block, axis, [(i, i ^ 1 << bit) for i in range(count)])  25.2 us
    ppermute x8, waiting for transfers between devices, on_device(): arrived = lax.ppermute(sends[step], 'row', across)  23.6 us
    ppermute x2, starting transfers between devices, mirrored(): got = got + lax.ppermute(halfway, ('row', 'col'), second)  20.5 us
    ppermute x12, starting transfers between devices, on_device(): here = here + lax.ppermute(carry[h], 'row', ring)  18.8 us
    ppermute x8, starting transfers between devices, on_device(): arrived = lax.ppermute(sends[step], 'row', across)  10.6 us
    ppermute x9, starting transfers between devices, swap_bit(): return lax.ppermute(block, axis, [(i, i ^ 1 << bit) for i in range(count)])  8.04 us
  transfers between devices with their start and end apart: 37, of which 15 were waited for; matrix products, arithmetic and copies ran while one was open for 2% of the time, Pallas kernels for 14%

profile of v1, /device:TPU:0, one launch (start us, length us, event | category | flops | bytes accessed | tf_op | source)
XLA Modules:
  0.0 178.7 jit_solution(18117438759163911766)
XLA Ops:
  1.8 3.1 %collective-permute-start.1 = (f32[1,64,1536]{2,1,0:T(8,128)S(1)}, f32[1,64,1536]{2,1,0:T(8,128)S(1)}, u32[]{:S(2)}, u32[]{:S(2)}) collective-permute-start(f32[1,64,1536]{2,1,0:T(8,128)S(1)} %get-tuple-element.45.refs_0_), channel_id=1, source_target_pairs={{0,2},{1,3},{2,0},{3,1},{4,6},{5,7},{6,4},{7,5},{8,10},{9,11},{10,... | collective-permute-start | bytes 1179656 | tf_op jit(solution)/shard_map/ppermute | solution.py:15
  5.4 9.4 %collective-permute-done.1.refs_2_ = f32[1,64,1536]{2,1,0:T(8,128)S(1)} collective-permute-done((f32[1,64,1536]{2,1,0:T(8,128)S(1)}, f32[1,64,1536]{2,1,0:T(8,128)S(1)}, u32[]{:S(2)}, u32[]{:S(2)}) %collective-permute-start.1) | collective-permute-done | bytes 393248 | tf_op jit(solution)/shard_map/ppermute | solution.py:15
  15.3 7.1 %collective-permute-done.18.refs_2_ = f32[1,64,1536]{2,1,0:T(8,128)S(1)} collective-permute-done((f32[1,64,1536]{2,1,0:T(8,128)S(1)}, f32[1,64,1536]{2,1,0:T(8,128)S(1)}, u32[]{:S(2)}, u32[]{:S(2)}) %collective-permute-start.18) | collective-permute-done | bytes 393248 | tf_op jit(solution)/shard_map/ppermute | solution.py:15
  22.5 12.7 %panel_terms.2 = (f32[1,2,32,1536]{3,2,1,0:T(8,128)S(1)}, f32[1,2,32,1536]{3,2,1,0:T(8,128)S(1)}, f32[1,2,32,1536]{3,2,1,0:T(8,128)S(1)}, f32[1,2,32,1536]{3,2,1,0:T(8,128)S(1)}, f32[4,1,2,32,1536]{4,3,2,1,0:T(8,128)S(1)}) custom-call(s32[2,8]{1,0:T(2,128)S(1)} %fusion.30.table_ref, s32[2,48]{1,0:T(2,128)S(1)} %copy-done, s32[2]{0:T(128)S(1)} %pad_add_fusion.1.place_ref, ...), custom_call_target="tpu_custom_call" | custom-call | flops 7247757312 | bytes 18874368 | tf_op jit(solution)/shard_map/panel_terms/pallas_call | solution.py:87
  39.3 12.7 %panel_terms.3 = (f32[1,2,32,1536]{3,2,1,0:T(8,128)S(1)}, f32[1,2,32,1536]{3,2,1,0:T(8,128)S(1)}, f32[1,2,32,1536]{3,2,1,0:T(8,128)S(1)}, f32[1,2,32,1536]{3,2,1,0:T(8,128)S(1)}, f32[4,1,2,32,1536]{4,3,2,1,0:T(8,128)S(1)}) custom-call(s32[2,8]{1,0:T(2,128)S(1)} %fusion.30.table_ref, s32[2,48]{1,0:T(2,128)S(1)} %copy-done, s32[2]{0:T(128)S(1)} %pad_add_fusion.1.place_ref, ...), custom_call_target="tpu_custom_call" | custom-call | flops 7247757312 | bytes 18874368 | tf_op jit(solution)/shard_map/panel_terms/pallas_call | solution.py:87
  53.8 3.7 %collective-permute-start.10 = (f32[1,32,1536]{2,1,0:T(8,128)S(1)}, f32[1,32,1536]{2,1,0:T(8,128)S(1)}, u32[]{:S(2)}, u32[]{:S(2)}) collective-permute-start(f32[1,32,1536]{2,1,0:T(8,128)S(1)} %get-tuple-element.33), channel_id=1, source_target_pairs={{8,0},{12,4},{16,8},{20,12},{24,16},{28,20},{0,24},{4,28},{9,1},{1... | collective-permute-start | bytes 589832 | tf_op jit(solution)/shard_map/ppermute | solution.py:236
  57.5 23.0 %collective-permute-done.23 = f32[1,2,32,1536]{3,2,1,0:T(8,128)S(1)} collective-permute-done((f32[1,2,32,1536]{3,2,1,0:T(8,128)S(1)}, f32[1,2,32,1536]{3,2,1,0:T(8,128)S(1)}, u32[]{:S(2)}, u32[]{:S(2)}) %collective-permute-start.23) | collective-permute-done | bytes 393248 | tf_op jit(solution)/shard_map/ppermute | solution.py:231
  85.5 4.6 %collective-permute-done.7 = f32[1,32,1536]{2,1,0:T(8,128)S(1)} collective-permute-done((f32[1,32,1536]{2,1,0:T(8,128)S(1)}, f32[1,32,1536]{2,1,0:T(8,128)S(1)}, u32[]{:S(2)}, u32[]{:S(2)}) %collective-permute-start.7) | collective-permute-done | bytes 196640 | tf_op jit(solution)/shard_map/ppermute | solution.py:236
  94.3 2.8 %collective-permute-start.11 = (f32[1,32,1536]{2,1,0:T(8,128)S(1)}, f32[1,32,1536]{2,1,0:T(8,128)S(1)}, u32[]{:S(2)}, u32[]{:S(2)}) collective-permute-start(f32[1,32,1536]{2,1,0:T(8,128)S(1)} %get-tuple-element.31), channel_id=1, source_target_pairs={{8,0},{12,4},{16,8},{20,12},{24,16},{28,20},{0,24},{4,28},{9,1},{1... | collective-permute-start | bytes 589832 | tf_op jit(solution)/shard_map/ppermute | solution.py:236
  100.2 2.1 %collective-permute-done.11 = f32[1,32,1536]{2,1,0:T(8,128)S(1)} collective-permute-done((f32[1,32,1536]{2,1,0:T(8,128)S(1)}, f32[1,32,1536]{2,1,0:T(8,128)S(1)}, u32[]{:S(2)}, u32[]{:S(2)}) %collective-permute-start.11) | collective-permute-done | bytes 196640 | tf_op jit(solution)/shard_map/ppermute | solution.py:236
  102.5 4.3 %collective-permute-done.8 = f32[1,32,1536]{2,1,0:T(8,128)S(1)} collective-permute-done((f32[1,32,1536]{2,1,0:T(8,128)S(1)}, f32[1,32,1536]{2,1,0:T(8,128)S(1)}, u32[]{:S(2)}, u32[]{:S(2)}) %collective-permute-start.8) | collective-permute-done | bytes 196640 | tf_op jit(solution)/shard_map/ppermute | solution.py:236
  106.8 2.4 %collective-permute-start.28 = (f32[1,32,1536]{2,1,0:T(8,128)S(1)}, f32[1,32,1536]{2,1,0:T(8,128)S(1)}, u32[]{:S(2)}, u32[]{:S(2)}) collective-permute-start(f32[1,32,1536]{2,1,0:T(8,128)S(1)} %get-tuple-element.37), channel_id=1, source_target_pairs={{8,0},{12,4},{16,8},{20,12},{24,16},{28,20},{0,24},{4,28},{9,1},{1... | collective-permute-start | bytes 589832 | tf_op jit(solution)/shard_map/ppermute | solution.py:236
  109.7 2.7 %collective-permute-done.25 = f32[1,32,1536]{2,1,0:T(8,128)S(1)} collective-permute-done((f32[1,32,1536]{2,1,0:T(8,128)S(1)}, f32[1,32,1536]{2,1,0:T(8,128)S(1)}, u32[]{:S(2)}, u32[]{:S(2)}) %collective-permute-start.25) | collective-permute-done | bytes 196640 | tf_op jit(solution)/shard_map/ppermute | solution.py:236
  112.4 3.2 %collective-permute-done.28 = f32[1,32,1536]{2,1,0:T(8,128)S(1)} collective-permute-done((f32[1,32,1536]{2,1,0:T(8,128)S(1)}, f32[1,32,1536]{2,1,0:T(8,128)S(1)}, u32[]{:S(2)}, u32[]{:S(2)}) %collective-permute-start.28) | collective-permute-done | bytes 196640 | tf_op jit(solution)/shard_map/ppermute | solution.py:236
  116.9 2.6 %collective-permute-start.29 = (f32[1,32,1536]{2,1,0:T(8,128)S(1)}, f32[1,32,1536]{2,1,0:T(8,128)S(1)}, u32[]{:S(2)}, u32[]{:S(2)}) collective-permute-start(f32[1,32,1536]{2,1,0:T(8,128)S(1)} %get-tuple-element.35), channel_id=1, source_target_pairs={{8,0},{12,4},{16,8},{20,12},{24,16},{28,20},{0,24},{4,28},{9,1},{1... | collective-permute-start | bytes 589832 | tf_op jit(solution)/shard_map/ppermute | solution.py:236
  119.5 7.6 %collective-permute-done.12 = f32[1,32,1536]{2,1,0:T(8,128)S(1)} collective-permute-done((f32[1,32,1536]{2,1,0:T(8,128)S(1)}, f32[1,32,1536]{2,1,0:T(8,128)S(1)}, u32[]{:S(2)}, u32[]{:S(2)}) %collective-permute-start.12) | collective-permute-done | bytes 196640 | tf_op jit(solution)/shard_map/ppermute | solution.py:236
  128.5 3.2 %collective-permute-start.13 = (f32[1,32,1536]{2,1,0:T(8,128)S(1)}, f32[1,32,1536]{2,1,0:T(8,128)S(1)}, u32[]{:S(2)}, u32[]{:S(2)}) collective-permute-start(f32[1,32,1536]{2,1,0:T(8,128)S(1)} %get-tuple-element.23), channel_id=1, source_target_pairs={{0,4},{1,12},{4,0},{5,8},{8,5},{9,13},{12,1},{13,9},{18,22},{19,30... | collective-permute-start | bytes 589832 | tf_op jit(solution)/shard_map/ppermute | solution.py:149
  133.1 2.9 %collective-permute-start.30 = (f32[1,32,1536]{2,1,0:T(8,128)S(1)}, f32[1,32,1536]{2,1,0:T(8,128)S(1)}, u32[]{:S(2)}, u32[]{:S(2)}) collective-permute-start(f32[1,32,1536]{2,1,0:T(8,128)S(1)} %get-tuple-element.26), channel_id=1, source_target_pairs={{0,4},{1,12},{4,0},{5,8},{8,5},{9,13},{12,1},{13,9},{18,22},{19,30... | collective-permute-start | bytes 589832 | tf_op jit(solution)/shard_map/ppermute | solution.py:149
  136.7 6.4 %collective-permute-start.15 = (f32[1,32,1536]{2,1,0:T(8,128)S(1)}, f32[1,32,1536]{2,1,0:T(8,128)S(1)}, u32[]{:S(2)}, u32[]{:S(2)}) collective-permute-start(f32[1,32,1536]{2,1,0:T(8,128)S(1)} %collective-permute-done.14), channel_id=1, source_target_pairs={{0,20},{1,28},{4,16},{5,24},{8,21},{9,29},{12,17},{13,25},{18,6},{... | collective-permute-start | bytes 589832 | tf_op jit(solution)/shard_map/ppermute | solution.py:152
  143.8 14.2 %collective-permute-start.32 = (f32[1,32,1536]{2,1,0:T(8,128)S(1)}, f32[1,32,1536]{2,1,0:T(8,128)S(1)}, u32[]{:S(2)}, u32[]{:S(2)}) collective-permute-start(f32[1,32,1536]{2,1,0:T(8,128)S(1)} %collective-permute-done.31), channel_id=1, source_target_pairs={{0,20},{1,28},{4,16},{5,24},{8,21},{9,29},{12,17},{13,25},{18,6},{... | collective-permute-start | bytes 589832 | tf_op jit(solution)/shard_map/ppermute | solution.py:152
  158.1 3.1 %collective-permute-done.32 = f32[1,32,1536]{2,1,0:T(8,128)S(1)} collective-permute-done((f32[1,32,1536]{2,1,0:T(8,128)S(1)}, f32[1,32,1536]{2,1,0:T(8,128)S(1)}, u32[]{:S(2)}, u32[]{:S(2)}) %collective-permute-start.32) | collective-permute-done | bytes 196640 | tf_op jit(solution)/shard_map/ppermute | solution.py:152
  164.0 4.0 %collective-permute-done.34 = f32[2,4,32,64]{3,2,1,0:T(8,128)S(1)} collective-permute-done((f32[2,4,32,64]{3,2,1,0:T(8,128)S(1)}, f32[2,4,32,64]{3,2,1,0:T(8,128)S(1)}, u32[]{:S(2)}, u32[]{:S(2)}) %collective-permute-start.34) | collective-permute-done | bytes 65568 | tf_op jit(solution)/shard_map/ppermute | solution.py:15
  169.1 3.7 %collective-permute-done.35 = f32[2,2,32,64]{3,2,1,0:T(8,128)S(1)} collective-permute-done((f32[2,2,32,64]{3,2,1,0:T(8,128)S(1)}, f32[2,2,32,64]{3,2,1,0:T(8,128)S(1)}, u32[]{:S(2)}, u32[]{:S(2)}) %collective-permute-start.35) | collective-permute-done | bytes 32800 | tf_op jit(solution)/shard_map/ppermute | solution.py:15
  172.8 3.4 %collective-permute-start.36 = (f32[2,1,32,64]{3,2,1,0:T(8,128)S(1)}, f32[2,1,32,64]{3,2,1,0:T(8,128)S(1)}, u32[]{:S(2)}, u32[]{:S(2)}) collective-permute-start(f32[2,1,32,64]{3,2,1,0:T(8,128)S(1)} %constant_dynamic-slice_fusion), channel_id=1, source_target_pairs={{0,16},{4,20},{8,24},{12,28},{16,0},{20,4},{24,8},{28,12},{1,17},{... | collective-permute-start | bytes 49160 | tf_op jit(solution)/shard_map/ppermute | solution.py:15
  (95 shorter events, 32.9 us)
Async XLA Ops:
  1.8 13.0 %collective-permute-start.1 = (f32[1,64,1536]{2,1,0:T(8,128)S(1)}, f32[1,64,1536]{2,1,0:T(8,128)S(1)}, u32[]{:S(2)}, u32[]{:S(2)}) collective-permute-start(f32[1,64,1536]{2,1,0:T(8,128)S(1)} %get-tuple-element.45.refs_0_), channel_id=1, source_target_pairs={{0,2},{1,3},{2,0},{3,1},{4,6},{5,7},{6,4},{7,5},{8,10},{9,11},{10,... | collective-permute-start | bytes 1179656 | tf_op jit(solution)/shard_map/ppermute | solution.py:15
  4.9 17.5 %collective-permute-start = (f32[1,64,1536]{2,1,0:T(8,128)S(1)}, f32[1,64,1536]{2,1,0:T(8,128)S(1)}, u32[]{:S(2)}, u32[]{:S(2)}) collective-permute-start(f32[1,64,1536]{2,1,0:T(8,128)S(1)} %get-tuple-element.45.refs_0_), channel_id=1, source_target_pairs={{0,1},{1,0},{2,3},{3,2},{4,5},{5,4},{6,7},{7,6},{8,9},{9,8},{10,11... | collective-permute-start | bytes 1179656 | tf_op jit(solution)/shard_map/ppermute | solution.py:15
  4.9 17.5 %collective-permute-start.18 = (f32[1,64,1536]{2,1,0:T(8,128)S(1)}, f32[1,64,1536]{2,1,0:T(8,128)S(1)}, u32[]{:S(2)}, u32[]{:S(2)}) collective-permute-start(f32[1,64,1536]{2,1,0:T(8,128)S(1)} %get-tuple-element.46.refs_0_), channel_id=1, source_target_pairs={{0,2},{1,3},{2,0},{3,1},{4,6},{5,7},{6,4},{7,5},{8,10},{9,11},{10,... | collective-permute-start | bytes 1179656 | tf_op jit(solution)/shard_map/ppermute | solution.py:15
  5.1 33.9 %collective-permute-start.17 = (f32[1,64,1536]{2,1,0:T(8,128)S(1)}, f32[1,64,1536]{2,1,0:T(8,128)S(1)}, u32[]{:S(2)}, u32[]{:S(2)}) collective-permute-start(f32[1,64,1536]{2,1,0:T(8,128)S(1)} %get-tuple-element.46.refs_0_), channel_id=1, source_target_pairs={{0,1},{1,0},{2,3},{3,2},{4,5},{5,4},{6,7},{7,6},{8,9},{9,8},{10,11... | collective-permute-start | bytes 1179656 | tf_op jit(solution)/shard_map/ppermute | solution.py:15
  22.4 16.9 %collective-permute-start.19 = (f32[1,64,1536]{2,1,0:T(8,128)S(1)}, f32[1,64,1536]{2,1,0:T(8,128)S(1)}, u32[]{:S(2)}, u32[]{:S(2)}) collective-permute-start(f32[1,64,1536]{2,1,0:T(8,128)S(1)} %collective-permute-done.18.refs_2_), channel_id=1, source_target_pairs={{0,1},{1,0},{2,3},{3,2},{4,5},{5,4},{6,7},{7,6},{8,9},{9,8},{10,11... | collective-permute-start | bytes 1179656 | tf_op jit(solution)/shard_map/ppermute | solution.py:15
  35.2 18.6 %collective-permute-start.6 = (f32[1,2,32,1536]{3,2,1,0:T(8,128)S(1)}, f32[1,2,32,1536]{3,2,1,0:T(8,128)S(1)}, u32[]{:S(2)}, u32[]{:S(2)}) collective-permute-start(f32[1,2,32,1536]{3,2,1,0:T(8,128)S(1)} %get-tuple-element.17), channel_id=1, source_target_pairs={{0,4},{4,0},{8,12},{12,8},{16,20},{20,16},{24,28},{28,24},{1,5},{5... | collective-permute-start | bytes 1179656 | tf_op jit(solution)/shard_map/ppermute | solution.py:231
  36.9 45.4 %collective-permute-start.5 = (f32[1,2,32,1536]{3,2,1,0:T(8,128)S(1)}, f32[1,2,32,1536]{3,2,1,0:T(8,128)S(1)}, u32[]{:S(2)}, u32[]{:S(2)}) collective-permute-start(f32[1,2,32,1536]{3,2,1,0:T(8,128)S(1)} %get-tuple-element.16), channel_id=1, source_target_pairs={{0,4},{4,0},{8,12},{12,8},{16,20},{20,16},{24,28},{28,24},{1,5},{5... | collective-permute-start | bytes 1179656 | tf_op jit(solution)/shard_map/ppermute | solution.py:231
  37.3 61.3 %collective-permute-start.4 = (f32[1,2,32,1536]{3,2,1,0:T(8,128)S(1)}, f32[1,2,32,1536]{3,2,1,0:T(8,128)S(1)}, u32[]{:S(2)}, u32[]{:S(2)}) collective-permute-start(f32[1,2,32,1536]{3,2,1,0:T(8,128)S(1)} %get-tuple-element.15), channel_id=1, source_target_pairs={{0,4},{4,0},{8,12},{12,8},{16,20},{20,16},{24,28},{28,24},{1,5},{5... | collective-permute-start | bytes 1179656 | tf_op jit(solution)/shard_map/ppermute | solution.py:231
  39.0 78.0 %collective-permute-start.3 = (f32[1,2,32,1536]{3,2,1,0:T(8,128)S(1)}, f32[1,2,32,1536]{3,2,1,0:T(8,128)S(1)}, u32[]{:S(2)}, u32[]{:S(2)}) collective-permute-start(f32[1,2,32,1536]{3,2,1,0:T(8,128)S(1)} %get-tuple-element.14), channel_id=1, source_target_pairs={{0,4},{4,0},{8,12},{12,8},{16,20},{20,16},{24,28},{28,24},{1,5},{5... | collective-permute-start | bytes 1179656 | tf_op jit(solution)/shard_map/ppermute | solution.py:231
  52.0 28.5 %collective-permute-start.23 = (f32[1,2,32,1536]{3,2,1,0:T(8,128)S(1)}, f32[1,2,32,1536]{3,2,1,0:T(8,128)S(1)}, u32[]{:S(2)}, u32[]{:S(2)}) collective-permute-start(f32[1,2,32,1536]{3,2,1,0:T(8,128)S(1)} %get-tuple-element.22), channel_id=1, source_target_pairs={{0,4},{4,0},{8,12},{12,8},{16,20},{20,16},{24,28},{28,24},{1,5},{5... | collective-permute-start | bytes 1179656 | tf_op jit(solution)/shard_map/ppermute | solution.py:231
  53.8 30.0 %collective-permute-start.10 = (f32[1,32,1536]{2,1,0:T(8,128)S(1)}, f32[1,32,1536]{2,1,0:T(8,128)S(1)}, u32[]{:S(2)}, u32[]{:S(2)}) collective-permute-start(f32[1,32,1536]{2,1,0:T(8,128)S(1)} %get-tuple-element.33), channel_id=1, source_target_pairs={{8,0},{12,4},{16,8},{20,12},{24,16},{28,20},{0,24},{4,28},{9,1},{1... | collective-permute-start | bytes 589832 | tf_op jit(solution)/shard_map/ppermute | solution.py:236
  82.3 10.4 %collective-permute-start.22 = (f32[1,2,32,1536]{3,2,1,0:T(8,128)S(1)}, f32[1,2,32,1536]{3,2,1,0:T(8,128)S(1)}, u32[]{:S(2)}, u32[]{:S(2)}) collective-permute-start(f32[1,2,32,1536]{3,2,1,0:T(8,128)S(1)} %get-tuple-element.21), channel_id=1, source_target_pairs={{0,4},{4,0},{8,12},{12,8},{16,20},{20,16},{24,28},{28,24},{1,5},{5... | collective-permute-start | bytes 1179656 | tf_op jit(solution)/shard_map/ppermute | solution.py:231
  92.8 16.5 %collective-permute-start.21 = (f32[1,2,32,1536]{3,2,1,0:T(8,128)S(1)}, f32[1,2,32,1536]{3,2,1,0:T(8,128)S(1)}, u32[]{:S(2)}, u32[]{:S(2)}) collective-permute-start(f32[1,2,32,1536]{3,2,1,0:T(8,128)S(1)} %get-tuple-element.20), channel_id=1, source_target_pairs={{0,4},{4,0},{8,12},{12,8},{16,20},{20,16},{24,28},{28,24},{1,5},{5... | collective-permute-start | bytes 1179656 | tf_op jit(solution)/shard_map/ppermute | solution.py:231
  98.5 33.2 %collective-permute-start.20 = (f32[1,2,32,1536]{3,2,1,0:T(8,128)S(1)}, f32[1,2,32,1536]{3,2,1,0:T(8,128)S(1)}, u32[]{:S(2)}, u32[]{:S(2)}) collective-permute-start(f32[1,2,32,1536]{3,2,1,0:T(8,128)S(1)} %get-tuple-element.19), channel_id=1, source_target_pairs={{0,4},{4,0},{8,12},{12,8},{16,20},{20,16},{24,28},{28,24},{1,5},{5... | collective-permute-start | bytes 1179656 | tf_op jit(solution)/shard_map/ppermute | solution.py:231
  109.3 17.8 %collective-permute-start.12 = (f32[1,32,1536]{2,1,0:T(8,128)S(1)}, f32[1,32,1536]{2,1,0:T(8,128)S(1)}, u32[]{:S(2)}, u32[]{:S(2)}) collective-permute-start(f32[1,32,1536]{2,1,0:T(8,128)S(1)} %get-tuple-element.29), channel_id=1, source_target_pairs={{8,0},{12,4},{16,8},{20,12},{24,16},{28,20},{0,24},{4,28},{9,1},{1... | collective-permute-start | bytes 589832 | tf_op jit(solution)/shard_map/ppermute | solution.py:236
  112.4 14.8 %collective-permute-start.9 = (f32[1,32,1536]{2,1,0:T(8,128)S(1)}, f32[1,32,1536]{2,1,0:T(8,128)S(1)}, u32[]{:S(2)}, u32[]{:S(2)}) collective-permute-start(f32[1,32,1536]{2,1,0:T(8,128)S(1)} %get-tuple-element.30), channel_id=1, source_target_pairs={{0,8},{4,12},{8,16},{12,20},{16,24},{20,28},{24,0},{28,4},{1,9},{5... | collective-permute-start | bytes 589832 | tf_op jit(solution)/shard_map/ppermute | solution.py:236
  115.7 16.0 %collective-permute-start.26 = (f32[1,32,1536]{2,1,0:T(8,128)S(1)}, f32[1,32,1536]{2,1,0:T(8,128)S(1)}, u32[]{:S(2)}, u32[]{:S(2)}) collective-permute-start(f32[1,32,1536]{2,1,0:T(8,128)S(1)} %get-tuple-element.36), channel_id=1, source_target_pairs={{0,8},{4,12},{8,16},{12,20},{16,24},{20,28},{24,0},{28,4},{1,9},{5... | collective-permute-start | bytes 589832 | tf_op jit(solution)/shard_map/ppermute | solution.py:236
  116.9 14.8 %collective-permute-start.29 = (f32[1,32,1536]{2,1,0:T(8,128)S(1)}, f32[1,32,1536]{2,1,0:T(8,128)S(1)}, u32[]{:S(2)}, u32[]{:S(2)}) collective-permute-start(f32[1,32,1536]{2,1,0:T(8,128)S(1)} %get-tuple-element.35), channel_id=1, source_target_pairs={{8,0},{12,4},{16,8},{20,12},{24,16},{28,20},{0,24},{4,28},{9,1},{1... | collective-permute-start | bytes 589832 | tf_op jit(solution)/shard_map/ppermute | solution.py:236
  128.5 29.5 %collective-permute-start.13 = (f32[1,32,1536]{2,1,0:T(8,128)S(1)}, f32[1,32,1536]{2,1,0:T(8,128)S(1)}, u32[]{:S(2)}, u32[]{:S(2)}) collective-permute-start(f32[1,32,1536]{2,1,0:T(8,128)S(1)} %get-tuple-element.23), channel_id=1, source_target_pairs={{0,4},{1,12},{4,0},{5,8},{8,5},{9,13},{12,1},{13,9},{18,22},{19,30... | collective-permute-start | bytes 589832 | tf_op jit(solution)/shard_map/ppermute | solution.py:149
  131.8 12.0 %collective-permute-start.31 = (f32[1,32,1536]{2,1,0:T(8,128)S(1)}, f32[1,32,1536]{2,1,0:T(8,128)S(1)}, u32[]{:S(2)}, u32[]{:S(2)}) collective-permute-start(f32[1,32,1536]{2,1,0:T(8,128)S(1)} %get-tuple-element.26), channel_id=1, source_target_pairs={{2,0},{3,1},{6,4},{7,5},{10,8},{11,9},{14,12},{15,13},{16,18},{17,... | collective-permute-start | bytes 589832 | tf_op jit(solution)/shard_map/ppermute | solution.py:151
  133.1 25.0 %collective-permute-start.30 = (f32[1,32,1536]{2,1,0:T(8,128)S(1)}, f32[1,32,1536]{2,1,0:T(8,128)S(1)}, u32[]{:S(2)}, u32[]{:S(2)}) collective-permute-start(f32[1,32,1536]{2,1,0:T(8,128)S(1)} %get-tuple-element.26), channel_id=1, source_target_pairs={{0,4},{1,12},{4,0},{5,8},{8,5},{9,13},{12,1},{13,9},{18,22},{19,30... | collective-permute-start | bytes 589832 | tf_op jit(solution)/shard_map/ppermute | solution.py:149
  136.7 21.3 %collective-permute-start.15 = (f32[1,32,1536]{2,1,0:T(8,128)S(1)}, f32[1,32,1536]{2,1,0:T(8,128)S(1)}, u32[]{:S(2)}, u32[]{:S(2)}) collective-permute-start(f32[1,32,1536]{2,1,0:T(8,128)S(1)} %collective-permute-done.14), channel_id=1, source_target_pairs={{0,20},{1,28},{4,16},{5,24},{8,21},{9,29},{12,17},{13,25},{18,6},{... | collective-permute-start | bytes 589832 | tf_op jit(solution)/shard_map/ppermute | solution.py:152
  143.1 14.9 %collective-permute-start.33 = (f32[1,32,1536]{2,1,0:T(8,128)S(1)}, f32[1,32,1536]{2,1,0:T(8,128)S(1)}, u32[]{:S(2)}, u32[]{:S(2)}) collective-permute-start(f32[1,32,1536]{2,1,0:T(8,128)S(1)} %broadcast_select_fusion.4), channel_id=1, source_target_pairs={{0,0},{1,8},{2,16},{3,24},{4,4},{5,12},{6,20},{7,28},{8,1},{9,9},{... | collective-permute-start | bytes 589832 | tf_op jit(solution)/shard_map/ppermute | solution.py:149
  143.8 17.3 %collective-permute-start.32 = (f32[1,32,1536]{2,1,0:T(8,128)S(1)}, f32[1,32,1536]{2,1,0:T(8,128)S(1)}, u32[]{:S(2)}, u32[]{:S(2)}) collective-permute-start(f32[1,32,1536]{2,1,0:T(8,128)S(1)} %collective-permute-done.31), channel_id=1, source_target_pairs={{0,20},{1,28},{4,16},{5,24},{8,21},{9,29},{12,17},{13,25},{18,6},{... | collective-permute-start | bytes 589832 | tf_op jit(solution)/shard_map/ppermute | solution.py:152
  (16 other events, 149.1 us)

commit v2 on v1

--- a/solution.py
+++ b/solution.py
@@ -29,14 +29,14 @@
 
 
 def terms_kernel(dims, table_ref, flags_ref, place_ref, inverse_ref, *refs):
-    pieces_count, ratio, narrow, steps, members, node, tile = dims
+    pieces_count, ratio, narrow, steps, members, node, tile, base = dims
     pieces, refs = refs[:pieces_count], refs[pieces_count:]
     sends, (kept_ref, high_ref, low_ref, left_ref) = refs[:steps], refs[steps:]
-    h = pl.program_id(0)
+    h = pl.program_id(0) + base
     n = pl.program_id(1)
     rows = members * steps * INNER * narrow
 
-    @pl.when((h == 0) & (n == 0))
+    @pl.when((pl.program_id(0) == 0) & (n == 0))
     def _():
         for m in range(pieces_count):
             for g in range(members):
@@ -73,7 +73,7 @@
                 kept_ref[j, g, 0, :, k : k + chunk] = total[g, j, 1, :, k : k + chunk] * factor
 
 
-def panel_terms(node, table, flags, place, inverse, pieces, ratio, tile):
+def panel_terms(node, table, flags, place, inverse, pieces, ratio, tile, halves):
     members, width, rows = pieces[0].shape
     count = len(pieces)
     steps = table.shape[1] // INNER
@@ -83,13 +83,13 @@
     tiles = half // block
     lefts = members * steps * INNER * narrow
     whole = pl.BlockSpec((members, width, rows), lambda h, n, table, flags, place: (0, 0, 0))
-    flops = 6 * lefts * inverse.size
+    flops = 3 * len(halves) * lefts * inverse.size
     outs = pl.pallas_call(
-        functools.partial(terms_kernel, (count, ratio, narrow, steps, members, node, tile)),
+        functools.partial(terms_kernel, (count, ratio, narrow, steps, members, node, tile, halves[0])),
         grid_spec=pltpu.PrefetchScalarGridSpec(
             num_scalar_prefetch=3,
-            grid=(2, tiles),
-            in_specs=[pl.BlockSpec((rows, block), lambda h, n, table, flags, place: (0, h * tiles + n))] + [whole] * count,
+            grid=(len(halves), tiles),
+            in_specs=[pl.BlockSpec((rows, block), lambda h, n, table, flags, place: (0, (h + halves[0]) * tiles + n))] + [whole] * count,
             out_specs=[pl.BlockSpec((members, 1, narrow, block), lambda h, n, table, flags, place: (0, h, 0, n))] * steps
             + [pl.BlockSpec((steps, members, 1, narrow, block), lambda h, n, table, flags, place: (0, 0, h, 0, n))],
             scratch_shapes=[
@@ -98,10 +98,10 @@
                 pltpu.VMEM((2 * lefts, rows), jnp.bfloat16),
             ],
         ),
-        out_shape=[jax.ShapeDtypeStruct((members, 2, narrow, half), jnp.float32)] * steps
-        + [jax.ShapeDtypeStruct((steps, members, 2, narrow, half), jnp.float32)],
-        compiler_params=pltpu.CompilerParams(vmem_limit_bytes=32 << 20),
-        cost_estimate=pl.CostEstimate(flops=flops, bytes_accessed=4 * inverse.size, transcendentals=0),
+        out_shape=[jax.ShapeDtypeStruct((members, len(halves), narrow, half), jnp.float32)] * steps
+        + [jax.ShapeDtypeStruct((steps, members, len(halves), narrow, half), jnp.float32)],
+        compiler_params=pltpu.CompilerParams(vmem_limit_bytes=(32 if len(halves) == 2 else 46) << 20),
+        cost_estimate=pl.CostEstimate(flops=flops, bytes_accessed=2 * len(halves) * inverse.size, transcendentals=0),
         name="panel_terms",
     )(table, flags, place, inverse, *pieces)
     return outs[:steps], outs[steps]
@@ -225,12 +225,23 @@
 
     row_results, col_results, diag_parts = [], [], []
     for s, pieces in enumerate(gathered):
-        sends, kept = panel_terms(s, table, ancestors, place, resident_inverse, pieces, ratio, tile)
+        terms = {}
+        for halves in [[0], [1]] if s == 0 else [[0, 1]]:
+            sends, kept = panel_terms(
+                s, table, ancestors, place, resident_inverse, pieces, ratio, tile, halves
+            )
+            for i, h in enumerate(halves):
+                terms[h] = (halves[0], i, sends, kept)
         carry = [None, None]
         for step in range(steps):
-            arrived = lax.ppermute(sends[step], "row", across)
+            came = {
+                base: lax.ppermute(sends[step], "row", across)
+                for base, _, sends, _ in terms.values()
+                if base == 0 or s == 0
+            }
             for h in range(2):
-                here = kept[step, :, h] + arrived[:, h]
+                base, i, _, kept = terms[h]
+                here = kept[step, :, i] + came[base][:, i]
                 if step:
                     ring = forward if h == 0 else backward
                     here = here + lax.ppermute(carry[h], "row", ring)

time: 179 us -> 188 us (1.050)
  waiting for transfers between devices: 77.6 us -> 95.5 us
  starting transfers between devices: 67.9 us -> 55.8 us
  Pallas kernels: 26.9 us -> 29.4 us
    ppermute x12, waiting for transfers between devices: 25.8 us -> 46.6 us  [on_device(): here = here + lax.ppermute(carry[h], 'row', ring)]
    ppermute x12, starting transfers between devices: 18.8 us -> 9.58 us  [on_device(): here = here + lax.ppermute(carry[h], 'row', ring)]
    ppermute x2, starting transfers between devices: 20.5 us -> 11.6 us  [mirrored(): got = got + lax.ppermute(halfway, ('row', 'col'), second)]
    ppermute x8 -> x12, waiting for transfers between devices: 23.6 us -> 18.3 us  [on_device(): lax.ppermute(sends[step], 'row', across)]
    ppermute x9, starting transfers between devices: 8.04 us -> 12 us  [swap_bit(): return lax.ppermute(block, axis, [(i, i ^ 1 << bit) for i in range(count)])]
    ppermute x2, waiting for transfers between devices: 3.07 us -> 6.04 us  [mirrored(): got = got + lax.ppermute(halfway, ('row', 'col'), second)]
    pallas_call x2 -> x3, Pallas kernels: 25.4 us -> 27.9 us  [panel_terms(): pl.pallas_call(functools.partial(terms_kernel, (count, ratio, narrow, ste...]
    ppermute x8 -> x12, starting transfers between devices: 10.6 us -> 12.9 us  [on_device(): lax.ppermute(sends[step], 'row', across)]
  transfers between devices with their start and end apart: 37 -> 41, of which waited for: 15 -> 20; matrix products, arithmetic and copies ran while one was open for 2% -> 2% of each run, Pallas kernels for 14% -> 15%
where the time goes in v2:
time: 188 us; the launch traced here: 187 us
  waiting for transfers between devices  95.5 us (51%)
  starting transfers between devices  55.8 us (30%)
  Pallas kernels  29.4 us (16%)
  other arithmetic  3.62 us (2%)
    ppermute x12, waiting for transfers between devices, on_device(): here = here + lax.ppermute(carry[h], 'row', ring)  46.6 us
    pallas_call x3, Pallas kernels, panel_terms(): pl.pallas_call(functools.partial(terms_kernel, (count, ratio, narrow, ste...  27.9 us
    ppermute x9, waiting for transfers between devices, swap_bit(): return lax.ppermute(block, axis, [(i, i ^ 1 << bit) for i in range(count)])  24.6 us
    ppermute x12, waiting for transfers between devices, on_device(): lax.ppermute(sends[step], 'row', across)  18.3 us
    ppermute x12, starting transfers between devices, on_device(): lax.ppermute(sends[step], 'row', across)  12.9 us
    ppermute x9, starting transfers between devices, swap_bit(): return lax.ppermute(block, axis, [(i, i ^ 1 << bit) for i in range(count)])  12 us
    ppermute x2, starting transfers between devices, mirrored(): got = got + lax.ppermute(halfway, ('row', 'col'), second)  11.6 us
    ppermute x12, starting transfers between devices, on_device(): here = here + lax.ppermute(carry[h], 'row', ring)  9.58 us
  transfers between devices with their start and end apart: 41, of which 20 were waited for; matrix products, arithmetic and copies ran while one was open for 2% of the time, Pallas kernels for 15%

profile of v2, /device:TPU:0, one launch (start us, length us, event | category | flops | bytes accessed | tf_op | source)
XLA Modules:
  0.0 186.8 jit_solution(12233404028640104245)
XLA Ops:
  1.8 3.1 %collective-permute-start.22 = (f32[1,64,1536]{2,1,0:T(8,128)S(1)}, f32[1,64,1536]{2,1,0:T(8,128)S(1)}, u32[]{:S(2)}, u32[]{:S(2)}) collective-permute-start(f32[1,64,1536]{2,1,0:T(8,128)S(1)} %get-tuple-element.50.refs_0_), channel_id=1, source_target_pairs={{0,2},{1,3},{2,0},{3,1},{4,6},{5,7},{6,4},{7,5},{8,10},{9,11},{10,... | collective-permute-start | bytes 1179656 | tf_op jit(solution)/shard_map/ppermute | solution.py:15
  5.5 9.3 %collective-permute-done.22.refs_2_ = f32[1,64,1536]{2,1,0:T(8,128)S(1)} collective-permute-done((f32[1,64,1536]{2,1,0:T(8,128)S(1)}, f32[1,64,1536]{2,1,0:T(8,128)S(1)}, u32[]{:S(2)}, u32[]{:S(2)}) %collective-permute-start.22) | collective-permute-done | bytes 393248 | tf_op jit(solution)/shard_map/ppermute | solution.py:15
  15.3 7.1 %collective-permute-done.1.refs_2_ = f32[1,64,1536]{2,1,0:T(8,128)S(1)} collective-permute-done((f32[1,64,1536]{2,1,0:T(8,128)S(1)}, f32[1,64,1536]{2,1,0:T(8,128)S(1)}, u32[]{:S(2)}, u32[]{:S(2)}) %collective-permute-start.1) | collective-permute-done | bytes 393248 | tf_op jit(solution)/shard_map/ppermute | solution.py:15
  22.5 12.7 %panel_terms.5 = (f32[1,2,32,1536]{3,2,1,0:T(8,128)S(1)}, f32[1,2,32,1536]{3,2,1,0:T(8,128)S(1)}, f32[1,2,32,1536]{3,2,1,0:T(8,128)S(1)}, f32[1,2,32,1536]{3,2,1,0:T(8,128)S(1)}, f32[4,1,2,32,1536]{4,3,2,1,0:T(8,128)S(1)}) custom-call(s32[2,8]{1,0:T(2,128)S(1)} %fusion.22.table_ref, s32[2,48]{1,0:T(2,128)S(1)} %copy-done, s32[2]{0:T(128)S(1)} %pad_add_fusion.1.place_ref, ...), custom_call_target="tpu_custom_call" | custom-call | flops 7247757312 | bytes 18874368 | tf_op jit(solution)/shard_map/panel_terms/pallas_call | solution.py:87
  39.0 7.6 %panel_terms.3 = (f32[1,1,32,1536]{3,2,1,0:T(8,128)S(1)}, f32[1,1,32,1536]{3,2,1,0:T(8,128)S(1)}, f32[1,1,32,1536]{3,2,1,0:T(8,128)S(1)}, f32[1,1,32,1536]{3,2,1,0:T(8,128)S(1)}, f32[4,1,1,32,1536]{4,3,2,1,0:T(8,128)S(1)}) custom-call(s32[2,8]{1,0:T(2,128)S(1)} %fusion.22.table_ref, s32[2,48]{1,0:T(2,128)S(1)} %copy-done, s32[2]{0:T(128)S(1)} %pad_add_fusion.1.place_ref, ...), custom_call_target="tpu_custom_call" | custom-call | flops 3623878656 | bytes 9437184 | tf_op jit(solution)/shard_map/panel_terms/pallas_call | solution.py:87
  48.7 7.6 %panel_terms.4 = (f32[1,1,32,1536]{3,2,1,0:T(8,128)S(1)}, f32[1,1,32,1536]{3,2,1,0:T(8,128)S(1)}, f32[1,1,32,1536]{3,2,1,0:T(8,128)S(1)}, f32[1,1,32,1536]{3,2,1,0:T(8,128)S(1)}, f32[4,1,1,32,1536]{4,3,2,1,0:T(8,128)S(1)}) custom-call(s32[2,8]{1,0:T(2,128)S(1)} %fusion.22.table_ref, s32[2,48]{1,0:T(2,128)S(1)} %copy-done, s32[2]{0:T(128)S(1)} %pad_add_fusion.1.place_ref, ...), custom_call_target="tpu_custom_call" | custom-call | flops 3623878656 | bytes 9437184 | tf_op jit(solution)/shard_map/panel_terms/pallas_call | solution.py:87
  56.3 12.0 %collective-permute-done.6 = f32[1,1,32,1536]{3,2,1,0:T(8,128)S(1)} collective-permute-done((f32[1,1,32,1536]{3,2,1,0:T(8,128)S(1)}, f32[1,1,32,1536]{3,2,1,0:T(8,128)S(1)}, u32[]{:S(2)}, u32[]{:S(2)}) %collective-permute-start.6) | collective-permute-done | bytes 196640 | tf_op jit(solution)/shard_map/ppermute | solution.py:238
  70.0 6.2 %collective-permute-done.13 = f32[1,1,32,1536]{3,2,1,0:T(8,128)S(1)} collective-permute-done((f32[1,1,32,1536]{3,2,1,0:T(8,128)S(1)}, f32[1,1,32,1536]{3,2,1,0:T(8,128)S(1)}, u32[]{:S(2)}, u32[]{:S(2)}) %collective-permute-start.13) | collective-permute-done | bytes 196640 | tf_op jit(solution)/shard_map/ppermute | solution.py:238
  80.3 5.8 %collective-permute-done.7 = f32[1,32,1536]{2,1,0:T(8,128)S(1)} collective-permute-done((f32[1,32,1536]{2,1,0:T(8,128)S(1)}, f32[1,32,1536]{2,1,0:T(8,128)S(1)}, u32[]{:S(2)}, u32[]{:S(2)}) %collective-permute-start.7) | collective-permute-done | bytes 196640 | tf_op jit(solution)/shard_map/ppermute | solution.py:247
  88.6 3.8 %collective-permute-done.14 = f32[1,32,1536]{2,1,0:T(8,128)S(1)} collective-permute-done((f32[1,32,1536]{2,1,0:T(8,128)S(1)}, f32[1,32,1536]{2,1,0:T(8,128)S(1)}, u32[]{:S(2)}, u32[]{:S(2)}) %collective-permute-start.14) | collective-permute-done | bytes 196640 | tf_op jit(solution)/shard_map/ppermute | solution.py:247
  92.9 8.8 %collective-permute-done.8 = f32[1,32,1536]{2,1,0:T(8,128)S(1)} collective-permute-done((f32[1,32,1536]{2,1,0:T(8,128)S(1)}, f32[1,32,1536]{2,1,0:T(8,128)S(1)}, u32[]{:S(2)}, u32[]{:S(2)}) %collective-permute-start.8) | collective-permute-done | bytes 196640 | tf_op jit(solution)/shard_map/ppermute | solution.py:247
  102.5 5.7 %collective-permute-done.15 = f32[1,32,1536]{2,1,0:T(8,128)S(1)} collective-permute-done((f32[1,32,1536]{2,1,0:T(8,128)S(1)}, f32[1,32,1536]{2,1,0:T(8,128)S(1)}, u32[]{:S(2)}, u32[]{:S(2)}) %collective-permute-start.15) | collective-permute-done | bytes 196640 | tf_op jit(solution)/shard_map/ppermute | solution.py:247
  108.4 6.5 %collective-permute-done.31 = f32[1,32,1536]{2,1,0:T(8,128)S(1)} collective-permute-done((f32[1,32,1536]{2,1,0:T(8,128)S(1)}, f32[1,32,1536]{2,1,0:T(8,128)S(1)}, u32[]{:S(2)}, u32[]{:S(2)}) %collective-permute-start.31) | collective-permute-done | bytes 196640 | tf_op jit(solution)/shard_map/ppermute | solution.py:247
  114.9 2.9 %collective-permute-done.28 = f32[1,32,1536]{2,1,0:T(8,128)S(1)} collective-permute-done((f32[1,32,1536]{2,1,0:T(8,128)S(1)}, f32[1,32,1536]{2,1,0:T(8,128)S(1)}, u32[]{:S(2)}, u32[]{:S(2)}) %collective-permute-start.28) | collective-permute-done | bytes 196640 | tf_op jit(solution)/shard_map/ppermute | solution.py:247
  123.8 2.6 %collective-permute-done.16 = f32[1,32,1536]{2,1,0:T(8,128)S(1)} collective-permute-done((f32[1,32,1536]{2,1,0:T(8,128)S(1)}, f32[1,32,1536]{2,1,0:T(8,128)S(1)}, u32[]{:S(2)}, u32[]{:S(2)}) %collective-permute-start.16) | collective-permute-done | bytes 196640 | tf_op jit(solution)/shard_map/ppermute | solution.py:247
  131.5 3.8 %collective-permute-start.33 = (f32[1,32,1536]{2,1,0:T(8,128)S(1)}, f32[1,32,1536]{2,1,0:T(8,128)S(1)}, u32[]{:S(2)}, u32[]{:S(2)}) collective-permute-start(f32[1,32,1536]{2,1,0:T(8,128)S(1)} %get-tuple-element.39), channel_id=1, source_target_pairs={{8,0},{12,4},{16,8},{20,12},{24,16},{28,20},{0,24},{4,28},{9,1},{1... | collective-permute-start | bytes 589832 | tf_op jit(solution)/shard_map/ppermute | solution.py:247
  136.0 5.1 %collective-permute-done.30 = f32[1,32,1536]{2,1,0:T(8,128)S(1)} collective-permute-done((f32[1,32,1536]{2,1,0:T(8,128)S(1)}, f32[1,32,1536]{2,1,0:T(8,128)S(1)}, u32[]{:S(2)}, u32[]{:S(2)}) %collective-permute-start.30) | collective-permute-done | bytes 196640 | tf_op jit(solution)/shard_map/ppermute | solution.py:247
  142.5 3.7 %collective-permute-start.34 = (f32[1,32,1536]{2,1,0:T(8,128)S(1)}, f32[1,32,1536]{2,1,0:T(8,128)S(1)}, u32[]{:S(2)}, u32[]{:S(2)}) collective-permute-start(f32[1,32,1536]{2,1,0:T(8,128)S(1)} %get-tuple-element.36), channel_id=1, source_target_pairs={{0,4},{1,12},{4,0},{5,8},{8,5},{9,13},{12,1},{13,9},{18,22},{19,30... | collective-permute-start | bytes 589832 | tf_op jit(solution)/shard_map/ppermute | solution.py:149
  147.5 9.0 %collective-permute-start.19 = (f32[1,32,1536]{2,1,0:T(8,128)S(1)}, f32[1,32,1536]{2,1,0:T(8,128)S(1)}, u32[]{:S(2)}, u32[]{:S(2)}) collective-permute-start(f32[1,32,1536]{2,1,0:T(8,128)S(1)} %collective-permute-done.18), channel_id=1, source_target_pairs={{0,20},{1,28},{4,16},{5,24},{8,21},{9,29},{12,17},{13,25},{18,6},{... | collective-permute-start | bytes 589832 | tf_op jit(solution)/shard_map/ppermute | solution.py:152
  157.2 2.6 %collective-permute-start.36 = (f32[1,32,1536]{2,1,0:T(8,128)S(1)}, f32[1,32,1536]{2,1,0:T(8,128)S(1)}, u32[]{:S(2)}, u32[]{:S(2)}) collective-permute-start(f32[1,32,1536]{2,1,0:T(8,128)S(1)} %collective-permute-done.35), channel_id=1, source_target_pairs={{0,20},{1,28},{4,16},{5,24},{8,21},{9,29},{12,17},{13,25},{18,6},{... | collective-permute-start | bytes 589832 | tf_op jit(solution)/shard_map/ppermute | solution.py:152
  161.8 4.1 %collective-permute-done.36 = f32[1,32,1536]{2,1,0:T(8,128)S(1)} collective-permute-done((f32[1,32,1536]{2,1,0:T(8,128)S(1)}, f32[1,32,1536]{2,1,0:T(8,128)S(1)}, u32[]{:S(2)}, u32[]{:S(2)}) %collective-permute-start.36) | collective-permute-done | bytes 196640 | tf_op jit(solution)/shard_map/ppermute | solution.py:152
  169.3 3.7 %collective-permute-done.38 = f32[2,4,32,64]{3,2,1,0:T(8,128)S(1)} collective-permute-done((f32[2,4,32,64]{3,2,1,0:T(8,128)S(1)}, f32[2,4,32,64]{3,2,1,0:T(8,128)S(1)}, u32[]{:S(2)}, u32[]{:S(2)}) %collective-permute-start.38) | collective-permute-done | bytes 65568 | tf_op jit(solution)/shard_map/ppermute | solution.py:15
  173.1 5.9 %collective-permute-start.39 = (f32[2,2,32,64]{3,2,1,0:T(8,128)S(1)}, f32[2,2,32,64]{3,2,1,0:T(8,128)S(1)}, u32[]{:S(2)}, u32[]{:S(2)}) collective-permute-start(f32[2,2,32,64]{3,2,1,0:T(8,128)S(1)} %dynamic-slice_bitcast_fusion.1), channel_id=1, source_target_pairs={{0,8},{4,12},{8,0},{12,4},{16,24},{20,28},{24,16},{28,20},{1,9},{5... | collective-permute-start | bytes 98312 | tf_op jit(solution)/shard_map/ppermute | solution.py:15
  183.1 3.0 %collective-permute-done.40 = f32[2,1,32,64]{3,2,1,0:T(8,128)S(1)} collective-permute-done((f32[2,1,32,64]{3,2,1,0:T(8,128)S(1)}, f32[2,1,32,64]{3,2,1,0:T(8,128)S(1)}, u32[]{:S(2)}, u32[]{:S(2)}) %collective-permute-start.40) | collective-permute-done | bytes 16416 | tf_op jit(solution)/shard_map/ppermute | solution.py:15
  (107 shorter events, 43.0 us)
Async XLA Ops:
  1.8 13.0 %collective-permute-start.22 = (f32[1,64,1536]{2,1,0:T(8,128)S(1)}, f32[1,64,1536]{2,1,0:T(8,128)S(1)}, u32[]{:S(2)}, u32[]{:S(2)}) collective-permute-start(f32[1,64,1536]{2,1,0:T(8,128)S(1)} %get-tuple-element.50.refs_0_), channel_id=1, source_target_pairs={{0,2},{1,3},{2,0},{3,1},{4,6},{5,7},{6,4},{7,5},{8,10},{9,11},{10,... | collective-permute-start | bytes 1179656 | tf_op jit(solution)/shard_map/ppermute | solution.py:15
  4.9 17.5 %collective-permute-start.21 = (f32[1,64,1536]{2,1,0:T(8,128)S(1)}, f32[1,64,1536]{2,1,0:T(8,128)S(1)}, u32[]{:S(2)}, u32[]{:S(2)}) collective-permute-start(f32[1,64,1536]{2,1,0:T(8,128)S(1)} %get-tuple-element.50.refs_0_), channel_id=1, source_target_pairs={{0,1},{1,0},{2,3},{3,2},{4,5},{5,4},{6,7},{7,6},{8,9},{9,8},{10,11... | collective-permute-start | bytes 1179656 | tf_op jit(solution)/shard_map/ppermute | solution.py:15
  4.9 34.1 %collective-permute-start = (f32[1,64,1536]{2,1,0:T(8,128)S(1)}, f32[1,64,1536]{2,1,0:T(8,128)S(1)}, u32[]{:S(2)}, u32[]{:S(2)}) collective-permute-start(f32[1,64,1536]{2,1,0:T(8,128)S(1)} %get-tuple-element.49.refs_0_), channel_id=1, source_target_pairs={{0,1},{1,0},{2,3},{3,2},{4,5},{5,4},{6,7},{7,6},{8,9},{9,8},{10,11... | collective-permute-start | bytes 1179656 | tf_op jit(solution)/shard_map/ppermute | solution.py:15
  5.4 17.0 %collective-permute-start.1 = (f32[1,64,1536]{2,1,0:T(8,128)S(1)}, f32[1,64,1536]{2,1,0:T(8,128)S(1)}, u32[]{:S(2)}, u32[]{:S(2)}) collective-permute-start(f32[1,64,1536]{2,1,0:T(8,128)S(1)} %get-tuple-element.49.refs_0_), channel_id=1, source_target_pairs={{0,2},{1,3},{2,0},{3,1},{4,6},{5,7},{6,4},{7,5},{8,10},{9,11},{10,... | collective-permute-start | bytes 1179656 | tf_op jit(solution)/shard_map/ppermute | solution.py:15
  22.4 16.6 %collective-permute-start.2 = (f32[1,64,1536]{2,1,0:T(8,128)S(1)}, f32[1,64,1536]{2,1,0:T(8,128)S(1)}, u32[]{:S(2)}, u32[]{:S(2)}) collective-permute-start(f32[1,64,1536]{2,1,0:T(8,128)S(1)} %collective-permute-done.1.refs_2_), channel_id=1, source_target_pairs={{0,1},{1,0},{2,3},{3,2},{4,5},{5,4},{6,7},{7,6},{8,9},{9,8},{10,11... | collective-permute-start | bytes 1179656 | tf_op jit(solution)/shard_map/ppermute | solution.py:15
  35.2 42.8 %collective-permute-start.27 = (f32[1,2,32,1536]{3,2,1,0:T(8,128)S(1)}, f32[1,2,32,1536]{3,2,1,0:T(8,128)S(1)}, u32[]{:S(2)}, u32[]{:S(2)}) collective-permute-start(f32[1,2,32,1536]{3,2,1,0:T(8,128)S(1)} %get-tuple-element.32), channel_id=1, source_target_pairs={{0,4},{4,0},{8,12},{12,8},{16,20},{20,16},{24,28},{28,24},{1,5},{5... | collective-permute-start | bytes 1179656 | tf_op jit(solution)/shard_map/ppermute | solution.py:238
  37.0 71.3 %collective-permute-start.26 = (f32[1,2,32,1536]{3,2,1,0:T(8,128)S(1)}, f32[1,2,32,1536]{3,2,1,0:T(8,128)S(1)}, u32[]{:S(2)}, u32[]{:S(2)}) collective-permute-start(f32[1,2,32,1536]{3,2,1,0:T(8,128)S(1)} %get-tuple-element.31), channel_id=1, source_target_pairs={{0,4},{4,0},{8,12},{12,8},{16,20},{20,16},{24,28},{28,24},{1,5},{5... | collective-permute-start | bytes 1179656 | tf_op jit(solution)/shard_map/ppermute | solution.py:238
  37.3 91.2 %collective-permute-start.25 = (f32[1,2,32,1536]{3,2,1,0:T(8,128)S(1)}, f32[1,2,32,1536]{3,2,1,0:T(8,128)S(1)}, u32[]{:S(2)}, u32[]{:S(2)}) collective-permute-start(f32[1,2,32,1536]{3,2,1,0:T(8,128)S(1)} %get-tuple-element.30), channel_id=1, source_target_pairs={{0,4},{4,0},{8,12},{12,8},{16,20},{20,16},{24,28},{28,24},{1,5},{5... | collective-permute-start | bytes 1179656 | tf_op jit(solution)/shard_map/ppermute | solution.py:238
  46.6 21.7 %collective-permute-start.6 = (f32[1,1,32,1536]{3,2,1,0:T(8,128)S(1)}, f32[1,1,32,1536]{3,2,1,0:T(8,128)S(1)}, u32[]{:S(2)}, u32[]{:S(2)}) collective-permute-start(f32[1,1,32,1536]{3,2,1,0:T(8,128)S(1)} %get-tuple-element.22), channel_id=1, source_target_pairs={{0,4},{4,0},{8,12},{12,8},{16,20},{20,16},{24,28},{28,24},{1,5},{5... | collective-permute-start | bytes 589832 | tf_op jit(solution)/shard_map/ppermute | solution.py:238
  47.0 32.7 %collective-permute-start.5 = (f32[1,1,32,1536]{3,2,1,0:T(8,128)S(1)}, f32[1,1,32,1536]{3,2,1,0:T(8,128)S(1)}, u32[]{:S(2)}, u32[]{:S(2)}) collective-permute-start(f32[1,1,32,1536]{3,2,1,0:T(8,128)S(1)} %get-tuple-element.21), channel_id=1, source_target_pairs={{0,4},{4,0},{8,12},{12,8},{16,20},{20,16},{24,28},{28,24},{1,5},{5... | collective-permute-start | bytes 589832 | tf_op jit(solution)/shard_map/ppermute | solution.py:238
  76.3 16.2 %collective-permute-start.4 = (f32[1,1,32,1536]{3,2,1,0:T(8,128)S(1)}, f32[1,1,32,1536]{3,2,1,0:T(8,128)S(1)}, u32[]{:S(2)}, u32[]{:S(2)}) collective-permute-start(f32[1,1,32,1536]{3,2,1,0:T(8,128)S(1)} %get-tuple-element.20), channel_id=1, source_target_pairs={{0,4},{4,0},{8,12},{12,8},{16,20},{20,16},{24,28},{28,24},{1,5},{5... | collective-permute-start | bytes 589832 | tf_op jit(solution)/shard_map/ppermute | solution.py:238
  87.9 31.6 %collective-permute-start.3 = (f32[1,1,32,1536]{3,2,1,0:T(8,128)S(1)}, f32[1,1,32,1536]{3,2,1,0:T(8,128)S(1)}, u32[]{:S(2)}, u32[]{:S(2)}) collective-permute-start(f32[1,1,32,1536]{3,2,1,0:T(8,128)S(1)} %get-tuple-element.19), channel_id=1, source_target_pairs={{0,4},{4,0},{8,12},{12,8},{16,20},{20,16},{24,28},{28,24},{1,5},{5... | collective-permute-start | bytes 589832 | tf_op jit(solution)/shard_map/ppermute | solution.py:238
  92.5 10.0 %collective-permute-start.11 = (f32[1,1,32,1536]{3,2,1,0:T(8,128)S(1)}, f32[1,1,32,1536]{3,2,1,0:T(8,128)S(1)}, u32[]{:S(2)}, u32[]{:S(2)}) collective-permute-start(f32[1,1,32,1536]{3,2,1,0:T(8,128)S(1)} %get-tuple-element.25), channel_id=1, source_target_pairs={{0,4},{4,0},{8,12},{12,8},{16,20},{20,16},{24,28},{28,24},{1,5},{5... | collective-permute-start | bytes 589832 | tf_op jit(solution)/shard_map/ppermute | solution.py:238
  102.5 12.4 %collective-permute-start.31 = (f32[1,32,1536]{2,1,0:T(8,128)S(1)}, f32[1,32,1536]{2,1,0:T(8,128)S(1)}, u32[]{:S(2)}, u32[]{:S(2)}) collective-permute-start(f32[1,32,1536]{2,1,0:T(8,128)S(1)} %get-tuple-element.43), channel_id=1, source_target_pairs={{8,0},{12,4},{16,8},{20,12},{24,16},{28,20},{0,24},{4,28},{9,1},{1... | collective-permute-start | bytes 589832 | tf_op jit(solution)/shard_map/ppermute | solution.py:247
  108.3 13.0 %collective-permute-start.10 = (f32[1,1,32,1536]{3,2,1,0:T(8,128)S(1)}, f32[1,1,32,1536]{3,2,1,0:T(8,128)S(1)}, u32[]{:S(2)}, u32[]{:S(2)}) collective-permute-start(f32[1,1,32,1536]{3,2,1,0:T(8,128)S(1)} %get-tuple-element.24), channel_id=1, source_target_pairs={{0,4},{4,0},{8,12},{12,8},{16,20},{20,16},{24,28},{28,24},{1,5},{5... | collective-permute-start | bytes 589832 | tf_op jit(solution)/shard_map/ppermute | solution.py:238
  119.4 15.9 %collective-permute-start.24 = (f32[1,2,32,1536]{3,2,1,0:T(8,128)S(1)}, f32[1,2,32,1536]{3,2,1,0:T(8,128)S(1)}, u32[]{:S(2)}, u32[]{:S(2)}) collective-permute-start(f32[1,2,32,1536]{3,2,1,0:T(8,128)S(1)} %get-tuple-element.29), channel_id=1, source_target_pairs={{0,4},{4,0},{8,12},{12,8},{16,20},{20,16},{24,28},{28,24},{1,5},{5... | collective-permute-start | bytes 1179656 | tf_op jit(solution)/shard_map/ppermute | solution.py:238
  126.4 33.4 %collective-permute-start.17 = (f32[1,32,1536]{2,1,0:T(8,128)S(1)}, f32[1,32,1536]{2,1,0:T(8,128)S(1)}, u32[]{:S(2)}, u32[]{:S(2)}) collective-permute-start(f32[1,32,1536]{2,1,0:T(8,128)S(1)} %get-tuple-element.33), channel_id=1, source_target_pairs={{0,4},{1,12},{4,0},{5,8},{8,5},{9,13},{12,1},{13,9},{18,22},{19,30... | collective-permute-start | bytes 589832 | tf_op jit(solution)/shard_map/ppermute | solution.py:149
  128.5 19.0 %collective-permute-start.18 = (f32[1,32,1536]{2,1,0:T(8,128)S(1)}, f32[1,32,1536]{2,1,0:T(8,128)S(1)}, u32[]{:S(2)}, u32[]{:S(2)}) collective-permute-start(f32[1,32,1536]{2,1,0:T(8,128)S(1)} %get-tuple-element.33), channel_id=1, source_target_pairs={{2,0},{3,1},{6,4},{7,5},{10,8},{11,9},{14,12},{15,13},{16,18},{17,... | collective-permute-start | bytes 589832 | tf_op jit(solution)/shard_map/ppermute | solution.py:151
  131.4 9.7 %collective-permute-start.30 = (f32[1,32,1536]{2,1,0:T(8,128)S(1)}, f32[1,32,1536]{2,1,0:T(8,128)S(1)}, u32[]{:S(2)}, u32[]{:S(2)}) collective-permute-start(f32[1,32,1536]{2,1,0:T(8,128)S(1)} %get-tuple-element.40), channel_id=1, source_target_pairs={{0,8},{4,12},{8,16},{12,20},{16,24},{20,28},{24,0},{28,4},{1,9},{5... | collective-permute-start | bytes 589832 | tf_op jit(solution)/shard_map/ppermute | solution.py:247
  131.5 11.0 %collective-permute-start.33 = (f32[1,32,1536]{2,1,0:T(8,128)S(1)}, f32[1,32,1536]{2,1,0:T(8,128)S(1)}, u32[]{:S(2)}, u32[]{:S(2)}) collective-permute-start(f32[1,32,1536]{2,1,0:T(8,128)S(1)} %get-tuple-element.39), channel_id=1, source_target_pairs={{8,0},{12,4},{16,8},{20,12},{24,16},{28,20},{0,24},{4,28},{9,1},{1... | collective-permute-start | bytes 589832 | tf_op jit(solution)/shard_map/ppermute | solution.py:247
  135.3 21.2 %collective-permute-start.20 = (f32[1,32,1536]{2,1,0:T(8,128)S(1)}, f32[1,32,1536]{2,1,0:T(8,128)S(1)}, u32[]{:S(2)}, u32[]{:S(2)}) collective-permute-start(f32[1,32,1536]{2,1,0:T(8,128)S(1)} %broadcast_select_fusion.8), channel_id=1, source_target_pairs={{0,0},{1,8},{2,16},{3,24},{4,4},{5,12},{6,20},{7,28},{8,1},{9,9},{... | collective-permute-start | bytes 589832 | tf_op jit(solution)/shard_map/ppermute | solution.py:149
  142.5 19.2 %collective-permute-start.34 = (f32[1,32,1536]{2,1,0:T(8,128)S(1)}, f32[1,32,1536]{2,1,0:T(8,128)S(1)}, u32[]{:S(2)}, u32[]{:S(2)}) collective-permute-start(f32[1,32,1536]{2,1,0:T(8,128)S(1)} %get-tuple-element.36), channel_id=1, source_target_pairs={{0,4},{1,12},{4,0},{5,8},{8,5},{9,13},{12,1},{13,9},{18,22},{19,30... | collective-permute-start | bytes 589832 | tf_op jit(solution)/shard_map/ppermute | solution.py:149
  146.2 11.0 %collective-permute-start.35 = (f32[1,32,1536]{2,1,0:T(8,128)S(1)}, f32[1,32,1536]{2,1,0:T(8,128)S(1)}, u32[]{:S(2)}, u32[]{:S(2)}) collective-permute-start(f32[1,32,1536]{2,1,0:T(8,128)S(1)} %get-tuple-element.36), channel_id=1, source_target_pairs={{2,0},{3,1},{6,4},{7,5},{10,8},{11,9},{14,12},{15,13},{16,18},{17,... | collective-permute-start | bytes 589832 | tf_op jit(solution)/shard_map/ppermute | solution.py:151
  147.5 14.2 %collective-permute-start.19 = (f32[1,32,1536]{2,1,0:T(8,128)S(1)}, f32[1,32,1536]{2,1,0:T(8,128)S(1)}, u32[]{:S(2)}, u32[]{:S(2)}) collective-permute-start(f32[1,32,1536]{2,1,0:T(8,128)S(1)} %collective-permute-done.18), channel_id=1, source_target_pairs={{0,20},{1,28},{4,16},{5,24},{8,21},{9,29},{12,17},{13,25},{18,6},{... | collective-permute-start | bytes 589832 | tf_op jit(solution)/shard_map/ppermute | solution.py:152
  (20 other events, 172.8 us)
